TPU v7x, 256 devices: a whole 4x4x8 slice. The times are simulated.
256 devices in a mesh: dp: 8 (over y, z_lo), seq: 32 (over x, z_hi, core).
Axes of the slice: x: 4, y: 4, z: 8 (z_hi: 4, z_lo: 2; z = z_hi * 2 + z_lo), core: 2. Of those that a mesh axis runs over, the one named last changes fastest.
Arguments:
- queries: bfloat16 [8, 4096, 2048], P('dp', 'seq'), may hold values from -6 to 6
- keys: bfloat16 [8, 4096, 2048], P('dp', 'seq'), may hold values from -6 to 6
- values: bfloat16 [8, 4096, 2048], P('dp', 'seq'), may hold values from -6 to 6
- frames: int32 [8, 4096], P('dp', 'seq'), may hold values from 0 to 340, never falling along the last dimension, each value on 1 to 16 neighbouring positions
- out_weight: bfloat16 [2048, 2048], P('seq'), may hold values from -0.125 to 0.125
- cotangent: bfloat16 [8, 4096, 2048], P('dp', 'seq'), may hold values from -6 to 6
Outputs:
- output: bfloat16 [8, 4096, 2048], P('dp', 'seq')
- grad_queries: bfloat16 [8, 4096, 2048], P('dp', 'seq')
- grad_keys: bfloat16 [8, 4096, 2048], P('dp', 'seq')
- grad_values: bfloat16 [8, 4096, 2048], P('dp', 'seq')
- grad_weight: float32 [2048, 2048], P('seq')
Inputs may be any that keep to these rules, and one draw needn't show every extreme that they name: `frames`: within each clip the frame index never falls along the tokens, starts at 0, and every frame 0 to 340 holds 1 to 16 consecutive tokens; some frame holds exactly 16.
All inputs are finite; a program needn't handle non-finite values.
Results may differ from a plain program's by a relative error of at most 0.022.
Values may be sent and summed in bfloat16 or wider, within the bound.
A program may use at most 128 MiB of HBM per device.

v0:
```python
import jax
import jax.numpy as jnp
from jax import lax
from jax.sharding import PartitionSpec as P

HS = 64


masked_score = -1e30


def sent_to_all(array, axis):
    copies = jnp.broadcast_to(array, (lax.axis_size(axis), *array.shape))
    return lax.all_to_all(copies, axis, split_axis=0, concat_axis=0, tiled=True)


def laid_out(blocks, dim):
    blocks = jnp.moveaxis(blocks, 0, dim)
    shape = blocks.shape
    return blocks.reshape(*shape[:dim], shape[dim] * shape[dim + 1], *shape[dim + 2 :])


def gather_directly(array, axis, dim):
    blocks = sent_to_all(array, axis)
    return laid_out(blocks, dim)


def of_everyone(array, axis):
    return sent_to_all(array, axis).astype(jnp.float32).sum(axis=0)


def side_by_side(arrays, axis, split_dim, concat_dim, along):
    both = jnp.concatenate(arrays, axis=along)
    result, at, done = (
        lax.all_to_all(both, axis, split_axis=split_dim, concat_axis=concat_dim, tiled=True),
        0,
        [],
    )
    for a in arrays:
        done.append(lax.slice_in_dim(result, at, at + a.shape[along], axis=along))
        at += a.shape[along]
    return tuple(done)


def key_blocks_needed(frame_all, query_frames, block_len, blocks_total):
    needed = jnp.sum((frame_all <= query_frames[-1]).astype(jnp.int32))
    return jnp.minimum((needed + block_len - 1) // block_len, blocks_total)


def block_scores(query_rows, query_frames, key_heads, frame_all, first_row, block_len):
    key_rows = lax.dynamic_slice_in_dim(key_heads, first_row, block_len, 0)
    key_frames = lax.dynamic_slice_in_dim(frame_all, first_row, block_len, 0)
    scores = jnp.einsum(
        "qhd,khd->hqk", query_rows, key_rows, preferred_element_type=jnp.float32
    ) * HS ** (-0.5)
    allowed = (key_frames[None, :] <= query_frames[:, None])[None]
    return (jnp.where(allowed, scores, masked_score), allowed, key_rows)


def add_rows(running, addition, first_row):
    current = lax.dynamic_slice_in_dim(running, first_row, addition.shape[0], 0)
    return lax.dynamic_update_slice_in_dim(running, current + addition, first_row, 0)


def forward_heads(head_items, frame_all):
    query_heads, key_heads, value_heads = head_items
    length_all = query_heads.shape[0]
    head_count = query_heads.shape[1]
    block_len = min(512, length_all)
    blocks_total = length_all // block_len

    def forward_one_block(block_index):
        first_row = block_index * block_len
        query_rows = lax.dynamic_slice_in_dim(query_heads, first_row, block_len, 0)
        query_frames = lax.dynamic_slice_in_dim(frame_all, first_row, block_len, 0)
        key_blocks = key_blocks_needed(frame_all, query_frames, block_len, blocks_total)

        def gather_stats(key_index, running):
            highest, exp_mass = running
            scores, allowed, key_rows = block_scores(
                query_rows, query_frames, key_heads, frame_all, key_index * block_len, block_len
            )
            new_high = jnp.maximum(highest, jnp.max(scores, axis=2))
            exp_terms = jnp.where(allowed, jnp.exp(scores - new_high[:, :, None]), 0.0)
            return (new_high, exp_mass * jnp.exp(highest - new_high) + jnp.sum(exp_terms, axis=2))

        start_stats = (
            jnp.full((head_count, block_len), masked_score, jnp.float32),
            jnp.zeros((head_count, block_len), jnp.float32),
        )
        highest, exp_mass = lax.fori_loop(0, key_blocks, gather_stats, start_stats)
        log_mass = highest + jnp.log(exp_mass)

        def accumulate(key_index, running):
            key_first = key_index * block_len
            scores, allowed, key_rows = block_scores(
                query_rows, query_frames, key_heads, frame_all, key_first, block_len
            )
            attn_weights = jnp.where(allowed, jnp.exp(scores - log_mass[:, :, None]), 0.0).astype(
                jnp.bfloat16
            )
            value_rows = lax.dynamic_slice_in_dim(value_heads, key_first, block_len, 0)
            return running + jnp.einsum(
                "hqk,khd->qhd", attn_weights, value_rows, preferred_element_type=jnp.float32
            )

        summed = lax.fori_loop(
            0, key_blocks, accumulate, jnp.zeros((block_len, head_count, HS), jnp.float32)
        )
        return (summed.astype(jnp.bfloat16), log_mass)

    attn_blocks, mass_blocks = lax.map(forward_one_block, jnp.arange(blocks_total, dtype=jnp.int32))
    attention = attn_blocks.reshape(length_all, head_count, HS)
    log_rows = jnp.swapaxes(mass_blocks, 1, 2).reshape(length_all, head_count)
    return (attention, log_rows, query_heads, key_heads, value_heads)


def backward_heads(
    query_heads, key_heads, value_heads, attn_heads, log_rows, grad_heads, frame_all
):
    length_all, head_count = log_rows.shape
    block_len = min(512, length_all)
    blocks_total = length_all // block_len
    score_scale = HS ** (-0.5)
    delta_all = jnp.sum(grad_heads.astype(jnp.float32) * attn_heads.astype(jnp.float32), axis=2)

    def backward_one_block(block_index, running):
        grad_query, grad_key, grad_value = running
        first_row = block_index * block_len
        query_rows = lax.dynamic_slice_in_dim(query_heads, first_row, block_len, 0)
        query_frames = lax.dynamic_slice_in_dim(frame_all, first_row, block_len, 0)
        grad_rows = lax.dynamic_slice_in_dim(grad_heads, first_row, block_len, 0)
        log_block = jnp.swapaxes(lax.dynamic_slice_in_dim(log_rows, first_row, block_len, 0), 0, 1)
        delta_block = jnp.swapaxes(
            lax.dynamic_slice_in_dim(delta_all, first_row, block_len, 0), 0, 1
        )
        key_blocks = key_blocks_needed(frame_all, query_frames, block_len, blocks_total)

        def per_key(key_index, state):
            query_sum, key_sum, value_sum = state
            key_first = key_index * block_len
            scores, allowed, key_rows = block_scores(
                query_rows, query_frames, key_heads, frame_all, key_first, block_len
            )
            value_rows = lax.dynamic_slice_in_dim(value_heads, key_first, block_len, 0)
            probabilities = jnp.where(allowed, jnp.exp(scores - log_block[:, :, None]), 0.0)
            value_part = jnp.einsum(
                "hqk,qhd->khd",
                probabilities.astype(jnp.bfloat16),
                grad_rows,
                preferred_element_type=jnp.float32,
            )
            grad_probs = jnp.einsum(
                "qhd,khd->hqk", grad_rows, value_rows, preferred_element_type=jnp.float32
            )
            grad_scores = (probabilities * (grad_probs - delta_block[:, :, None])).astype(
                jnp.bfloat16
            )
            query_sum = query_sum + jnp.einsum(
                "hqk,khd->qhd", grad_scores, key_rows, preferred_element_type=jnp.float32
            )
            key_part = jnp.einsum(
                "hqk,qhd->khd", grad_scores, query_rows, preferred_element_type=jnp.float32
            )
            return (
                query_sum,
                add_rows(key_sum, key_part, key_first),
                add_rows(value_sum, value_part, key_first),
            )

        query_sum, grad_key, grad_value = lax.fori_loop(
            0,
            key_blocks,
            per_key,
            (jnp.zeros((block_len, head_count, HS), jnp.float32), grad_key, grad_value),
        )
        query_done = (query_sum * score_scale).astype(jnp.bfloat16)
        grad_query = lax.dynamic_update_slice_in_dim(grad_query, query_done, first_row, 0)
        return (grad_query, grad_key, grad_value)

    start_state = (
        jnp.zeros((length_all, head_count, HS), jnp.bfloat16),
        jnp.zeros((length_all, head_count, HS), jnp.float32),
        jnp.zeros((length_all, head_count, HS), jnp.float32),
    )
    grad_query, grad_key, grad_value = lax.fori_loop(
        0, blocks_total, backward_one_block, start_state
    )
    return (
        grad_query,
        (grad_key * score_scale).astype(jnp.bfloat16),
        grad_value.astype(jnp.bfloat16),
    )


def on_device(queries, keys, values, frames, out_weight, cotangent):
    tok_count = queries.shape[1]
    head_width = queries.shape[2]
    head_count = head_width // HS
    group_count = lax.axis_size("seq")
    frame_all = gather_directly(frames, "seq", 1)[0]

    def split_heads(source):
        return source[0].reshape(tok_count, group_count, head_count // group_count, HS)

    query_items = lax.all_to_all(
        split_heads(queries), "seq", split_axis=1, concat_axis=0, tiled=True
    )
    key_items = lax.all_to_all(split_heads(keys), "seq", split_axis=1, concat_axis=0, tiled=True)
    value_items = lax.all_to_all(
        split_heads(values), "seq", split_axis=1, concat_axis=0, tiled=True
    )
    results = forward_heads((query_items[:, 0], key_items[:, 0], value_items[:, 0]), frame_all)
    attn_four, log_three, query_four, key_four, value_four = tuple(
        (item[:, None] for item in results)
    )
    attn_heads = attn_four[:, 0]
    log_rows = log_three[:, 0]
    query_heads = query_four[:, 0]
    key_heads = key_four[:, 0]
    value_heads = value_four[:, 0]
    length_all = attn_heads.shape[0]
    local_heads = attn_heads.shape[1]
    attn_time = lax.all_to_all(attn_heads, "seq", split_axis=0, concat_axis=1, tiled=True).reshape(
        tok_count, head_width
    )
    grad_out = cotangent[0]
    out_sum = jnp.dot(
        attn_time,
        lax.all_gather(out_weight, "seq", axis=0, tiled=True),
        preferred_element_type=jnp.float32,
    )
    attn_flat = attn_heads.reshape(length_all, local_heads * HS)
    shard_rows = lax.all_gather(grad_out, "seq", axis=0, tiled=True)
    weight_sum = lax.dot_general(
        attn_flat, shard_rows, (((0,), (0,)), ((), ())), preferred_element_type=jnp.float32
    )
    part_value = lax.dot_general(
        shard_rows, out_weight, (((1,), (1,)), ((), ())), preferred_element_type=jnp.float32
    )
    grad_sum = part_value
    grad_part, grad_sum = (weight_sum, grad_sum)
    grad_heads = grad_sum.astype(jnp.bfloat16).reshape(length_all, local_heads, HS)
    grad_weight = of_everyone(grad_part.astype(jnp.bfloat16), "dp").astype(jnp.float32)
    query_grad, key_grad, value_grad = backward_heads(
        query_heads, key_heads, value_heads, attn_heads, log_rows, grad_heads, frame_all
    )
    query_time, key_time, value_time = side_by_side(
        (query_grad, key_grad, value_grad), "seq", 0, 1, 2
    )
    output = out_sum.astype(jnp.bfloat16)[None]
    return (
        output,
        query_time.reshape(tok_count, head_width)[None],
        key_time.reshape(tok_count, head_width)[None],
        value_time.reshape(tok_count, head_width)[None],
        grad_weight,
    )


def solution(mesh):
    in_specs = (
        P("dp", "seq", None),
        P("dp", "seq", None),
        P("dp", "seq", None),
        P("dp", "seq"),
        P("seq", None),
        P("dp", "seq", None),
    )
    out_specs = (
        P("dp", "seq", None),
        P("dp", "seq", None),
        P("dp", "seq", None),
        P("dp", "seq", None),
        P("seq", None),
    )
    return jax.shard_map(
        on_device, mesh=mesh, in_specs=in_specs, out_specs=out_specs, check_vma=False
    )
```

profile of v0, /device:TPU:1, one launch (start us, length us, event | category | flops | bytes accessed | tf_op | source)
XLA Modules:
  0.0 484.7 jit_solution(6819803231690237616)
XLA Ops:
  10.0 12.6 %all-to-all-start.1 = ((bf16[128,32,1,64]{0,3,2,1:T(8,128)(2,1)}), bf16[128,32,1,64]{0,3,2,1:T(8,128)(2,1)S(1)}, u32[]{:S(2)}, u32[]{:S(2)}) async-start(bf16[128,32,1,64]{0,3,2,1:T(8,128)(2,1)} %bitcast.37), calls=%async_computation.1 | async-start | bytes 1048576 | tf_op jit(solution)/shard_map/all_to_all | solution.py:206
  24.6 19.0 %all-to-all-done.1 = bf16[128,32,1,64]{0,3,2,1:T(8,128)(2,1)S(1)} async-done(((bf16[128,32,1,64]{0,3,2,1:T(8,128)(2,1)}), bf16[128,32,1,64]{0,3,2,1:T(8,128)(2,1)S(1)}, u32[]{:S(2)}, u32[]{:S(2)}) %all-to-all-start.1) | async-done | bytes 524320 | tf_op jit(solution)/shard_map/all_to_all | solution.py:206
  43.6 7.1 %all-to-all-start.2 = ((bf16[128,32,1,64]{0,3,2,1:T(8,128)(2,1)}), bf16[128,32,1,64]{0,3,2,1:T(8,128)(2,1)S(1)}, u32[]{:S(2)}, u32[]{:S(2)}) async-start(bf16[128,32,1,64]{0,3,2,1:T(8,128)(2,1)} %bitcast.41), calls=%async_computation.2 | async-start | bytes 1048576 | tf_op jit(solution)/shard_map/all_to_all | solution.py:209
  50.9 18.7 %all-to-all-done.2 = bf16[128,32,1,64]{0,3,2,1:T(8,128)(2,1)S(1)} async-done(((bf16[128,32,1,64]{0,3,2,1:T(8,128)(2,1)}), bf16[128,32,1,64]{0,3,2,1:T(8,128)(2,1)S(1)}, u32[]{:S(2)}, u32[]{:S(2)}) %all-to-all-start.2) | async-done | bytes 524320 | tf_op jit(solution)/shard_map/all_to_all | solution.py:209
  69.6 34.2 %all_to_all.88 = bf16[128,32,1,64]{0,3,2,1:T(8,128)(2,1)S(1)} all-to-all(bf16[128,32,1,64]{0,3,2,1:T(8,128)(2,1)S(1)} %bitcast.285), channel_id=1, replica_groups=mesh['dp'=8,'seq'=32] {'seq'}, dimensions={1} | all-to-all | bytes 1048576 | tf_op jit(solution)/shard_map/all_to_all | solution.py:210
  104.4 4.9 %all-to-all-start = ((s32[32,1,128]{2,1,0:T(1,128)}), s32[32,1,128]{2,1,0:T(1,128)S(1)}, u32[]{:S(2)}, u32[]{:S(2)}) async-start(s32[32,1,128]{2,1,0:T(1,128)} %broadcast_in_dim.72), calls=%async_computation | async-start | bytes 32768 | tf_op jit(solution)/shard_map/all_to_all | solution.py:14
  111.8 7.3 %all-to-all-done = s32[32,1,128]{2,1,0:T(1,128)S(1)} async-done(((s32[32,1,128]{2,1,0:T(1,128)}), s32[32,1,128]{2,1,0:T(1,128)S(1)}, u32[]{:S(2)}, u32[]{:S(2)}) %all-to-all-start) | async-done | bytes 16416 | tf_op jit(solution)/shard_map/all_to_all | solution.py:14
  119.1 92.7 %while.163 = (s32[]{:T(128)}, bf16[8,512,1,64]{1,3,2,0:T(8,128)(2,1)S(1)}, f32[8,1,512]{2,1,0:T(1,128)S(1)}, s32[8]{0:T(128)S(1)}, s32[4096]{0:T(1024)S(1)}, /*i...) while((s32[]{:T(128)}, ...), condition=%wide.region_8.9_spmd, body=%wide.region_0.8_spmd.sunk | while | flops 104412704 | bytes 3229739 | solution.py:112
  129.9 2.2 while.166
  138.2 2.9 while.166
  141.2 2.8 while.167
  148.0 3.7 while.166
  151.7 3.5 while.167
  159.2 3.7 while.166
  162.9 3.5 while.167
  170.4 5.1 %while.166 = (s32[]{:T(128)}, f32[1,512]{1,0:T(1,128)S(1)}, f32[1,512]{1,0:T(1,128)S(1)}, s32[]{:T(128)}, s32[4096]{0:T(1024)S(1)}, /*index=5*/s32[512]{0:T(512)...) while((s32[]{:T(128)}, f32[1,512]{1,0:T(1,128)S(1)}, ...), condition=%wide.region_5.5_spmd, body=%wide.region_2.4_spmd.sunk | while | flops 35652612 | bytes 2267307 | solution.py:91
  175.6 5.0 %while.167 = (s32[]{:T(128)}, f32[512,1,64]{0,2,1:T(8,128)S(1)}, s32[]{:T(128)}, bf16[4096,1,64]{0,2,1:T(8,128)(2,1)S(1)}, s32[4096]{0:T(1024)S(1)}, /*index=5*/...) while((s32[]{:T(128)}, f32[512,1,64]{0,2,1:T(8,128)S(1)}, ...), condition=%wide.region_7.7_spmd, body=%wide.region_6.6_spmd.sunk | while | flops 68714504 | bytes 470191 | solution.py:107
  184.5 5.9 %while.166 = (s32[]{:T(128)}, f32[1,512]{1,0:T(1,128)S(1)}, f32[1,512]{1,0:T(1,128)S(1)}, s32[]{:T(128)}, s32[4096]{0:T(1024)S(1)}, /*index=5*/s32[512]{0:T(512)...) while((s32[]{:T(128)}, f32[1,512]{1,0:T(1,128)S(1)}, ...), condition=%wide.region_5.5_spmd, body=%wide.region_2.4_spmd.sunk | while | flops 35652612 | bytes 2267307 | solution.py:91
  190.5 5.7 %while.167 = (s32[]{:T(128)}, f32[512,1,64]{0,2,1:T(8,128)S(1)}, s32[]{:T(128)}, bf16[4096,1,64]{0,2,1:T(8,128)(2,1)S(1)}, s32[4096]{0:T(1024)S(1)}, /*index=5*/...) while((s32[]{:T(128)}, f32[512,1,64]{0,2,1:T(8,128)S(1)}, ...), condition=%wide.region_7.7_spmd, body=%wide.region_6.6_spmd.sunk | while | flops 68714504 | bytes 470191 | solution.py:107
  200.1 5.9 %while.166 = (s32[]{:T(128)}, f32[1,512]{1,0:T(1,128)S(1)}, f32[1,512]{1,0:T(1,128)S(1)}, s32[]{:T(128)}, s32[4096]{0:T(1024)S(1)}, /*index=5*/s32[512]{0:T(512)...) while((s32[]{:T(128)}, f32[1,512]{1,0:T(1,128)S(1)}, ...), condition=%wide.region_5.5_spmd, body=%wide.region_2.4_spmd.sunk | while | flops 35652612 | bytes 2267307 | solution.py:91
  206.0 5.7 %while.167 = (s32[]{:T(128)}, f32[512,1,64]{0,2,1:T(8,128)S(1)}, s32[]{:T(128)}, bf16[4096,1,64]{0,2,1:T(8,128)(2,1)S(1)}, s32[4096]{0:T(1024)S(1)}, /*index=5*/...) while((s32[]{:T(128)}, f32[512,1,64]{0,2,1:T(8,128)S(1)}, ...), condition=%wide.region_7.7_spmd, body=%wide.region_6.6_spmd.sunk | while | flops 68714504 | bytes 470191 | solution.py:107
  214.0 5.8 %reshape.117 = bf16[4096,1,64]{2,1,0:T(2,128)(2,1)S(1)} reshape(bf16[8,512,1,64]{3,1,0,2:T(8,128)(2,1)} %copy.113) | data formatting | bytes 1048576 | tf_op jit(solution)/shard_map/squeeze;broadcast_in_dim;reshape | solution.py:217
  220.3 23.5 %reduce.6 = bf16[4096,64]{1,0:T(8,128)(2,1)} reduce(bf16[4096,1,64]{2,1,0:T(2,128)(2,1)S(1)} %reshape.117, bf16[]{:T(256)} %broadcast.111), dimensions={1}, to_apply=%reshape.117.reduce_sub_computation | reduce | bytes 1048578 | tf_op jit(solution)/shard_map/squeeze;broadcast_in_dim;reshape | solution.py:217
  243.8 3.0 reshape.118
  246.8 4.7 all-to-all-start.4
  251.6 11.8 %multiply_reduce_fusion = (f32[4096]{0:T(1024)S(1)}, bf16[4096,64]{0,1:T(8,128)(2,1)}) fusion(bf16[4096,64]{0,1:T(8,128)(2,1)} %bitcast.274, bf16[64,2048]{1,0:T(8,128)(2,1)S(1)} %copy-done.5, bf16[1,4096,2048]{2,1,0:T(8,128)(2,1)} %all-gather.6.cloned.1.call-done), kind=kOutput, calls=%fused_computation.91 | convolution fusion | flops 1075048448 | bytes 18104320 | tf_op jit(solution)/shard_map/dot_general | solution.py:238
  264.3 105.6 %while.165 = (s32[]{:T(128)}, bf16[4096,1,64]{0,2,1:T(8,128)(2,1)}, f32[4096,1,64]{0,2,1:T(8,128)S(1)}, f32[4096,1,64]{0,2,1:T(8,128)S(1)}, s32[4096]{0:T(1024)S...) while((s32[]{:T(128)}, bf16[4096,1,64]{0,2,1:T(8,128)(2,1)}, ...), condition=%wide.region_14.15_spmd, body=%wide.region_10.14_spmd.sunk | while | flops 170307600 | bytes 6595400 | solution.py:186
  268.0 3.4 while.168
  275.8 5.1 %while.168 = (s32[]{:T(128)}, f32[512,1,64]{0,2,1:T(8,128)S(1)}, f32[4096,1,64]{0,2,1:T(8,128)S(1)}, f32[4096,1,64]{0,2,1:T(8,128)S(1)}, s32[]{:T(128)}, /*index...) while((s32[]{:T(128)}, f32[512,1,64]{0,2,1:T(8,128)S(1)}, ...), condition=%wide.region_13.13_spmd, body=%wide.region_12.12_spmd.sunk | while | flops 170229760 | bytes 5976291 | solution.py:171
  285.2 6.7 %while.168 = (s32[]{:T(128)}, f32[512,1,64]{0,2,1:T(8,128)S(1)}, f32[4096,1,64]{0,2,1:T(8,128)S(1)}, f32[4096,1,64]{0,2,1:T(8,128)S(1)}, s32[]{:T(128)}, /*index...) while((s32[]{:T(128)}, f32[512,1,64]{0,2,1:T(8,128)S(1)}, ...), condition=%wide.region_13.13_spmd, body=%wide.region_12.12_spmd.sunk | while | flops 170229760 | bytes 5976291 | solution.py:171
  296.3 8.4 %while.168 = (s32[]{:T(128)}, f32[512,1,64]{0,2,1:T(8,128)S(1)}, f32[4096,1,64]{0,2,1:T(8,128)S(1)}, f32[4096,1,64]{0,2,1:T(8,128)S(1)}, s32[]{:T(128)}, /*index...) while((s32[]{:T(128)}, f32[512,1,64]{0,2,1:T(8,128)S(1)}, ...), condition=%wide.region_13.13_spmd, body=%wide.region_12.12_spmd.sunk | while | flops 170229760 | bytes 5976291 | solution.py:171
  309.0 8.4 %while.168 = (s32[]{:T(128)}, f32[512,1,64]{0,2,1:T(8,128)S(1)}, f32[4096,1,64]{0,2,1:T(8,128)S(1)}, f32[4096,1,64]{0,2,1:T(8,128)S(1)}, s32[]{:T(128)}, /*index...) while((s32[]{:T(128)}, f32[512,1,64]{0,2,1:T(8,128)S(1)}, ...), condition=%wide.region_13.13_spmd, body=%wide.region_12.12_spmd.sunk | while | flops 170229760 | bytes 5976291 | solution.py:171
  321.8 11.8 %while.168 = (s32[]{:T(128)}, f32[512,1,64]{0,2,1:T(8,128)S(1)}, f32[4096,1,64]{0,2,1:T(8,128)S(1)}, f32[4096,1,64]{0,2,1:T(8,128)S(1)}, s32[]{:T(128)}, /*index...) while((s32[]{:T(128)}, f32[512,1,64]{0,2,1:T(8,128)S(1)}, ...), condition=%wide.region_13.13_spmd, body=%wide.region_12.12_spmd.sunk | while | flops 170229760 | bytes 5976291 | solution.py:171
  338.0 13.5 %while.168 = (s32[]{:T(128)}, f32[512,1,64]{0,2,1:T(8,128)S(1)}, f32[4096,1,64]{0,2,1:T(8,128)S(1)}, f32[4096,1,64]{0,2,1:T(8,128)S(1)}, s32[]{:T(128)}, /*index...) while((s32[]{:T(128)}, f32[512,1,64]{0,2,1:T(8,128)S(1)}, ...), condition=%wide.region_13.13_spmd, body=%wide.region_12.12_spmd.sunk | while | flops 170229760 | bytes 5976291 | solution.py:171
  355.8 13.5 %while.168 = (s32[]{:T(128)}, f32[512,1,64]{0,2,1:T(8,128)S(1)}, f32[4096,1,64]{0,2,1:T(8,128)S(1)}, f32[4096,1,64]{0,2,1:T(8,128)S(1)}, s32[]{:T(128)}, /*index...) while((s32[]{:T(128)}, f32[512,1,64]{0,2,1:T(8,128)S(1)}, ...), condition=%wide.region_13.13_spmd, body=%wide.region_12.12_spmd.sunk | while | flops 170229760 | bytes 5976291 | solution.py:171
  371.1 2.5 reduce.7
  373.6 3.1 copy.119
  376.8 3.3 reshape.120
  380.1 9.9 %all-to-all-start.5 = ((bf16[32,2,12288]{2,1,0:T(2,128)(2,1)}), bf16[32,2,12288]{2,1,0:T(2,128)(2,1)S(1)}, u32[]{:S(2)}, u32[]{:S(2)}) async-start(bf16[32,2,12288]{2,1,0:T(2,128)(2,1)} %reshape.120), calls=%async_computation.5 | async-start | bytes 3145728 | tf_op jit(solution)/shard_map/all_to_all | solution.py:35
  390.0 8.8 %fusion.72 = bf16[64,2048]{1,0:T(8,128)(2,1)S(1)} fusion(bf16[4096,64]{0,1:T(8,128)(2,1)S(1)} %bitcast.275, bf16[1,4096,2048]{2,1,0:T(8,128)(2,1)} %all-gather.6.cloned.1.call-done), kind=kOutput, calls=%fused_computation.88 | convolution fusion | flops 1073872896 | bytes 17563648 | tf_op jit(solution)/shard_map/dot_general | solution.py:235
  398.8 24.2 %all-to-all-done.5 = bf16[32,2,12288]{2,1,0:T(2,128)(2,1)S(1)} async-done(((bf16[32,2,12288]{2,1,0:T(2,128)(2,1)}), bf16[32,2,12288]{2,1,0:T(2,128)(2,1)S(1)}, u32[]{:S(2)}, u32[]{:S(2)}) %all-to-all-start.5) | async-done | bytes 1572896 | tf_op jit(solution)/shard_map/all_to_all | solution.py:35
  424.9 16.4 %all-to-all-start.6 = ((bf16[8,64,2048]{2,1,0:T(8,128)(2,1)}), bf16[8,64,2048]{2,1,0:T(8,128)(2,1)}, u32[]{:S(2)}, u32[]{:S(2)}) async-start(bf16[8,64,2048]{2,1,0:T(8,128)(2,1)} %broadcast_in_dim.75), calls=%async_computation.6 | async-start | bytes 4194304 | tf_op jit(solution)/shard_map/all_to_all | solution.py:14
  441.3 4.1 reshape.119
  445.4 2.3 copy.102
  448.1 5.6 %fusion.71 = bf16[1,128,2048]{2,1,0:T(8,128)(2,1)} fusion(bf16[128,2048]{0,1:T(8,128)(2,1)S(1)} %bitcast.279, bf16[2048,2048]{1,0:T(8,128)(2,1)} %all-gather.4.cloned.1.call-done), kind=kOutput, calls=%fused_computation.87 | convolution fusion | flops 1074003968 | bytes 9437184 | tf_op jit(solution)/shard_map/dot_general | solution.py:228
  453.6 7.2 %reshape.121 = bf16[4096,1,192]{2,1,0:T(2,128)(2,1)} reshape(bf16[32,2,12288]{2,1,0:T(2,128)(2,1)S(1)} %copy-done.2) | data formatting | bytes 3145728
  460.9 9.9 %copy.106 = bf16[4096,1,192]{0,2,1:T(8,128)(2,1)S(1)} copy(bf16[4096,1,192]{2,1,0:T(2,128)(2,1)} %reshape.121) | data formatting | bytes 3145728 | tf_op jit(solution)/shard_map/all_to_all | solution.py:35
  475.0 2.8 convert_reduce_fusion.2
  (784 shorter events, 200.1 us)
Async XLA Ops:
  7.2 43.5 %copy-start.6 = (bf16[1,128,2048]{2,1,0:T(8,128)(2,1)S(1)}, bf16[1,128,2048]{2,1,0:T(8,128)(2,1)}, u32[]{:S(2)}) copy-start(bf16[1,128,2048]{2,1,0:T(8,128)(2,1)} %param.18) | copy-start | bytes 1572868
  7.2 244.4 %all-gather.6.cloned.1.call-start = ((), (), s32[]{:S(2)}) async-start(), calls=%async_computation.8 | async-start | bytes 17301504 | tf_op jit(solution)/shard_map/all_gather | solution.py:234
  7.9 95.9 %copy-start.7 = (s32[1,128]{1,0:T(1,128)S(1)}, s32[1,128]{1,0:T(1,128)}, u32[]{:S(2)}) copy-start(s32[1,128]{1,0:T(1,128)} %param.19) | copy-start | bytes 1540
  10.0 33.6 %all-to-all-start.1 = ((bf16[128,32,1,64]{0,3,2,1:T(8,128)(2,1)}), bf16[128,32,1,64]{0,3,2,1:T(8,128)(2,1)S(1)}, u32[]{:S(2)}, u32[]{:S(2)}) async-start(bf16[128,32,1,64]{0,3,2,1:T(8,128)(2,1)} %bitcast.37), calls=%async_computation.1 | async-start | bytes 1048576 | tf_op jit(solution)/shard_map/all_to_all | solution.py:206
  43.6 26.0 %all-to-all-start.2 = ((bf16[128,32,1,64]{0,3,2,1:T(8,128)(2,1)}), bf16[128,32,1,64]{0,3,2,1:T(8,128)(2,1)S(1)}, u32[]{:S(2)}, u32[]{:S(2)}) async-start(bf16[128,32,1,64]{0,3,2,1:T(8,128)(2,1)} %bitcast.41), calls=%async_computation.2 | async-start | bytes 1048576 | tf_op jit(solution)/shard_map/all_to_all | solution.py:209
  104.4 14.7 %all-to-all-start = ((s32[32,1,128]{2,1,0:T(1,128)}), s32[32,1,128]{2,1,0:T(1,128)S(1)}, u32[]{:S(2)}, u32[]{:S(2)}) async-start(s32[32,1,128]{2,1,0:T(1,128)} %broadcast_in_dim.72), calls=%async_computation | async-start | bytes 32768 | tf_op jit(solution)/shard_map/all_to_all | solution.py:14
  109.3 338.8 %all-gather.4.cloned.1.call-start = ((), (), s32[]{:S(2)}) async-start(), calls=%async_computation.7 | async-start | bytes 8650752 | tf_op jit(solution)/shard_map/all_gather | solution.py:230
  211.7 1.4 copy-start.3
  219.8 31.8 %copy-start.5 = (bf16[64,2048]{1,0:T(8,128)(2,1)S(1)}, bf16[64,2048]{1,0:T(8,128)(2,1)}, u32[]{:S(2)}) copy-start(bf16[64,2048]{1,0:T(8,128)(2,1)} %param.20) | copy-start | bytes 786436
  246.8 133.3 %all-to-all-start.4 = ((bf16[32,2,4096]{2,1,0:T(2,128)(2,1)}), bf16[32,2,4096]{2,1,0:T(2,128)(2,1)}, u32[]{:S(2)}, u32[]{:S(2)}) async-start(bf16[32,2,4096]{2,1,0:T(2,128)(2,1)} %reshape.118), calls=%async_computation.4 | async-start | bytes 1048576 | tf_op jit(solution)/shard_map/all_to_all | solution.py:224
  369.9 1.0 copy-start.4
  376.8 13.2 %copy-start = (bf16[8,8,8,512]{3,1,2,0:T(8,128)(2,1)S(1)}, bf16[8,8,8,512]{3,1,2,0:T(8,128)(2,1)}, u32[]{:S(2)}) copy-start(bf16[8,8,8,512]{3,1,2,0:T(8,128)(2,1)} %copy.116) | copy-start | bytes 1572868
  380.1 43.0 %all-to-all-start.5 = ((bf16[32,2,12288]{2,1,0:T(2,128)(2,1)}), bf16[32,2,12288]{2,1,0:T(2,128)(2,1)S(1)}, u32[]{:S(2)}, u32[]{:S(2)}) async-start(bf16[32,2,12288]{2,1,0:T(2,128)(2,1)} %reshape.120), calls=%async_computation.5 | async-start | bytes 3145728 | tf_op jit(solution)/shard_map/all_to_all | solution.py:35
  423.1 1.8 copy-start.1
  424.9 50.1 %all-to-all-start.6 = ((bf16[8,64,2048]{2,1,0:T(8,128)(2,1)}), bf16[8,64,2048]{2,1,0:T(8,128)(2,1)}, u32[]{:S(2)}, u32[]{:S(2)}) async-start(bf16[8,64,2048]{2,1,0:T(8,128)(2,1)} %broadcast_in_dim.75), calls=%async_computation.6 | async-start | bytes 4194304 | tf_op jit(solution)/shard_map/all_to_all | solution.py:14
  448.0 5.6 %copy-start.2 = (bf16[32,2,12288]{2,1,0:T(2,128)(2,1)S(1)}, bf16[32,2,12288]{2,1,0:T(2,128)(2,1)}, u32[]{:S(2)}) copy-start(bf16[32,2,12288]{2,1,0:T(2,128)(2,1)} %copy-done.1) | copy-start | bytes 4718596
Sparse Core Ops, SparseCore 0:
  10.5 141.3 all-gather.5
  154.5 74.9 all-gather.3
where the time goes:
time: 488 us; the launch traced here: 485 us
  matrix products  131 us (27%)
  local copies, waits for them, and re-layouts  89.7 us (18%)
  waiting for transfers between devices  70.4 us (14%)
  other arithmetic  66.4 us (14%)
  starting transfers between devices  55.8 us (11%)
  blocking collectives  34.2 us (7%)
  loops' own time  22.7 us (5%)
  between operations  14.4 us (3%)
    all_to_all x1, blocking collectives, on_device(): lax.all_to_all(split_heads(values), 'seq', split_axis=1, concat_axis=0, t...  34.2 us
    dot_general x84, matrix products, block_scores(): jnp.einsum('qhd,khd->hqk', query_rows, key_rows, preferred_element_type=j...  33.1 us
    unnamed x30, local copies, waits for them, and re-layouts  30.5 us
    dot_general x42, matrix products, accumulate(): jnp.einsum('hqk,khd->qhd', attn_weights, value_rows, preferred_element_ty...  25.1 us
    all_to_all x1, waiting for transfers between devices, side_by_side(): lax.all_to_all(both, axis, split_axis=split_dim, concat_axis=concat_dim,...  24.2 us
    another operation x1, other arithmetic, on_device(): attn_heads = attn_four[:, 0]  23.5 us
    all_to_all x2, starting transfers between devices, sent_to_all(): return lax.all_to_all(copies, axis, split_axis=0, concat_axis=0, tiled=True)  21.2 us
    reduce_sum x16, other arithmetic, key_blocks_needed(): needed = jnp.sum((frame_all <= query_frames[-1]).astype(jnp.int32))  20.9 us
  transfers between devices with their start and end apart: 8, of which 4 were waited for; matrix products, arithmetic and copies ran while one was open for 58% of the time, Pallas kernels for 0%

commit v1 on v0

v1 whole, which is shorter than its diff:
```python
import jax
import jax.numpy as jnp
from jax import lax
from jax.experimental import pallas as pl
from jax.experimental.pallas import tpu as pltpu
from jax.sharding import PartitionSpec as P

HS = 64
QB = 512
QH = 256
KT = 512
TAIL = 16
NEG = -1e30
f32, bf = jnp.float32, jnp.bfloat16
VM = pl.BlockSpec(memory_space=pltpu.VMEM)


def dg(a, b, ca, cb):
    return lax.dot_general(a, b, (((ca,), (cb,)), ((), ())), preferred_element_type=f32)


def pack_qkv_kernel(q_ref, k_ref, v_ref, out_ref):
    tok = q_ref.shape[0]
    half = tok // 2
    for h in range(q_ref.shape[1] // HS):
        cols = slice(h * HS, (h + 1) * HS)
        out_ref[h, 0:tok, 0:HS] = q_ref[:, cols]
        out_ref[h, 0:tok, HS : 2 * HS] = k_ref[:, cols]
        out_ref[h, tok : tok + half, 0:HS] = v_ref[0:half, cols]
        out_ref[h, tok : tok + half, HS : 2 * HS] = v_ref[half:tok, cols]


def unpack_qkv_kernel(in_ref, q_ref, k_ref, v_ref):
    tok = q_ref.shape[0]
    half = tok // 2
    for h in range(q_ref.shape[1] // HS):
        cols = slice(h * HS, (h + 1) * HS)
        q_ref[:, cols] = in_ref[h, 0:tok, 0:HS]
        k_ref[:, cols] = in_ref[h, 0:tok, HS : 2 * HS]
        v_ref[0:half, cols] = in_ref[h, tok : tok + half, 0:HS]
        v_ref[half:tok, cols] = in_ref[h, tok : tok + half, HS : 2 * HS]


def grad_attention_kernel(cot_ref, w_ref, out_ref):
    tok = cot_ref.shape[0]
    half = tok // 2
    step = 4 * HS
    for c in range(w_ref.shape[0] // step):
        part = dg(cot_ref[...], w_ref[c * step : (c + 1) * step, :], 1, 1).astype(bf)
        for i in range(4):
            cols = slice(i * HS, (i + 1) * HS)
            out_ref[4 * c + i, :, 0:HS] = part[0:half, cols]
            out_ref[4 * c + i, :, HS : 2 * HS] = part[half:tok, cols]


def output_kernel(o_ref, w_ref, cot_ref, out_ref, gw_ref, att):
    tok = out_ref.shape[0]
    half = tok // 2
    for h in range(o_ref.shape[0]):
        cols = slice(h * HS, (h + 1) * HS)
        att[0:half, cols] = o_ref[h, :, 0:HS]
        att[half:tok, cols] = o_ref[h, :, HS : 2 * HS]
    width = w_ref.shape[1]
    for c in range(width // 512):
        cols = slice(c * 512, (c + 1) * 512)
        out_ref[:, cols] = dg(att[...], w_ref[:, cols], 1, 0).astype(bf)
    for c in range(att.shape[1] // 256):
        rows = slice(c * 256, (c + 1) * 256)
        gw_ref[rows, :] = dg(att[:, rows], cot_ref[...], 0, 0).astype(bf)


def unpack_heads(a_ref, qp, kp, vp):
    tok = 2 * a_ref.shape[1] // 3
    half = tok // 2
    length = a_ref.shape[0] * tok
    scale = jnp.asarray(HS**-0.5, bf)

    def one(t, c):
        first = pl.multiple_of(t * tok, tok)
        qp[pl.ds(first, tok), :] = a_ref[t, 0:tok, 0:HS] * scale
        kp[pl.ds(first, tok), :] = a_ref[t, 0:tok, HS : 2 * HS]
        vp[pl.ds(first, half), :] = a_ref[t, tok : tok + half, 0:HS]
        vp[pl.ds(first + half, half), :] = a_ref[t, tok : tok + half, HS : 2 * HS]
        return c

    lax.fori_loop(0, a_ref.shape[0], one, 0)
    kp[length : length + TAIL, :] = jnp.zeros((TAIL, HS), bf)
    vp[length : length + TAIL, :] = jnp.zeros((TAIL, HS), bf)


def fwd_kernel(a_ref, end_ref, o_ref, lse_ref, qp, kp, vp, acc, ml):
    unpack_heads(a_ref, qp, kp, vp)
    tok = 2 * a_ref.shape[1] // 3
    half = tok // 2
    length = a_ref.shape[0] * tok

    def tile(qh, h, k0, n, end):
        s = dg(kp[pl.ds(k0, n), :], qh, 1, 1)
        if end is not None:
            pos = lax.broadcasted_iota(jnp.int32, (n, QH), 0) + k0
            s = jnp.where(pos < end, s, NEG)
        m = ml[2 * h : 2 * h + 1, :]
        mn = jnp.maximum(m, jnp.max(s, axis=0, keepdims=True))
        p = jnp.exp(s - mn)
        al = jnp.exp(m - mn)
        ml[2 * h : 2 * h + 1, :] = mn
        ml[2 * h + 1 : 2 * h + 2, :] = ml[2 * h + 1 : 2 * h + 2, :] * al + jnp.sum(
            p, axis=0, keepdims=True
        )
        acc[h] = acc[h] * al + dg(vp[pl.ds(k0, n), :], p.astype(bf), 0, 0)

    def qblock(b, c):
        qs = pl.multiple_of(b * QB, QB)
        qh = [qp[pl.ds(qs + h * QH, QH), :] for h in range(2)]
        for h in range(2):
            ml[2 * h : 2 * h + 1, :] = jnp.full((1, QH), NEG, f32)
            ml[2 * h + 1 : 2 * h + 2, :] = jnp.zeros((1, QH), f32)
            acc[h] = jnp.zeros((HS, QH), f32)

        def kb(j, c):
            for h in range(2):
                tile(qh[h], h, pl.multiple_of(j * KT, KT), KT, None)
            return c

        lax.fori_loop(0, b, kb, 0)
        for h in range(2):
            tile(qh[h], h, qs, (h + 1) * QH + TAIL, end_ref[0:1, pl.ds(qs + h * QH, QH)])
        for h in range(2):
            total = ml[2 * h + 1 : 2 * h + 2, :]
            o = (acc[h] / total).T.astype(bf)
            for i in range(QH // tok):
                t = (QB // tok) * b + (QH // tok) * h + i
                o_ref[t, :, 0:HS] = o[i * tok : i * tok + half, :]
                o_ref[t, :, HS : 2 * HS] = o[i * tok + half : (i + 1) * tok, :]
            lse_ref[0:1, pl.ds(qs + h * QH, QH)] = ml[2 * h : 2 * h + 1, :] + jnp.log(total)
        return c

    lax.fori_loop(0, length // QB, qblock, 0)


def bwd_kernel(a_ref, do_ref, o_ref, end_ref, lse_ref, g_ref, qp, kp, vp, dqa, dka, dva):
    unpack_heads(a_ref, qp, kp, vp)
    tok = 2 * a_ref.shape[1] // 3
    half = tok // 2
    length = a_ref.shape[0] * tok
    dka[...] = jnp.zeros_like(dka)
    dva[...] = jnp.zeros_like(dva)

    def tile(qh, do, lse, dl, h, k0, n, end):
        r = pl.ds(k0, n)
        kk = kp[r, :]
        p = jnp.exp(dg(kk, qh, 1, 1) - lse)
        if end is not None:
            pos = lax.broadcasted_iota(jnp.int32, (n, QH), 0) + k0
            p = jnp.where(pos < end, p, 0.0)
        dp = dg(vp[r, :], do, 1, 1)
        dva[r, :] = dva[r, :] + dg(p.astype(bf), do, 1, 0)
        ds = (p * (dp - dl)).astype(bf)
        dka[r, :] = dka[r, :] + dg(ds, qh, 1, 0)
        dqa[h] = dqa[h] + dg(kk, ds, 0, 0)

    def halves(ref, t0):
        parts = []
        for i in range(QH // tok):
            parts.append(ref[t0 + i, :, 0:HS])
            parts.append(ref[t0 + i, :, HS : 2 * HS])
        return jnp.concatenate(parts, axis=0)

    def qblock(b, c):
        qs = pl.multiple_of(b * QB, QB)
        qh, do, lse, dl = [], [], [], []
        for h in range(2):
            r = pl.ds(qs + h * QH, QH)
            t0 = (QB // tok) * b + (QH // tok) * h
            qh.append(qp[r, :])
            do.append(halves(do_ref, t0))
            prod = do[h].astype(f32) * halves(o_ref, t0).astype(f32)
            dl.append(jnp.sum(prod.T, axis=0, keepdims=True))
            lse.append(lse_ref[0:1, r])
            dqa[h] = jnp.zeros((HS, QH), f32)

        def kb(j, c):
            for h in range(2):
                tile(qh[h], do[h], lse[h], dl[h], h, pl.multiple_of(j * KT, KT), KT, None)
            return c

        lax.fori_loop(0, b, kb, 0)
        for h in range(2):
            end = end_ref[0:1, pl.ds(qs + h * QH, QH)]
            tile(qh[h], do[h], lse[h], dl[h], h, qs, (h + 1) * QH + TAIL, end)
        for h in range(2):
            dq = (dqa[h] * (HS**-0.5)).T.astype(bf)
            for i in range(QH // tok):
                t = (QB // tok) * b + (QH // tok) * h + i
                g_ref[t, 0:tok, 0:HS] = dq[i * tok : (i + 1) * tok, :]
        return c

    lax.fori_loop(0, length // QB, qblock, 0)

    def finish(t, c):
        first = pl.multiple_of(t * tok, tok)
        g_ref[t, 0:tok, HS : 2 * HS] = dka[pl.ds(first, tok), :].astype(bf)
        g_ref[t, tok : tok + half, 0:HS] = dva[pl.ds(first, half), :].astype(bf)
        g_ref[t, tok : tok + half, HS : 2 * HS] = dva[pl.ds(first + half, half), :].astype(bf)
        return c

    lax.fori_loop(0, a_ref.shape[0], finish, 0)


def call(kernel, name, outs, args, scratch=(), flops=0, nbytes=0):
    return pl.pallas_call(
        kernel,
        out_shape=outs,
        in_specs=[VM] * len(args),
        out_specs=jax.tree.map(lambda _: VM, outs),
        scratch_shapes=list(scratch),
        compiler_params=pltpu.CompilerParams(vmem_limit_bytes=48 << 20),
        cost_estimate=pl.CostEstimate(flops=flops, bytes_accessed=nbytes, transcendentals=0),
        name=name,
    )(*args)


def exchange(array, axis):
    return lax.all_to_all(array, axis, split_axis=0, concat_axis=0, tiled=True)


def on_device(queries, keys, values, frames, out_weight, cotangent):
    tok, width = queries.shape[1], queries.shape[2]
    group = lax.axis_size("seq")
    length = tok * group
    sds = jax.ShapeDtypeStruct
    half = tok // 2

    packed = call(
        pack_qkv_kernel,
        "pack_qkv",
        sds((group, tok + half, 2 * HS), bf),
        (queries[0], keys[0], values[0]),
        nbytes=6 * tok * width,
    )
    heads = exchange(packed, "seq")
    weight = lax.all_gather(out_weight, "seq", axis=0, tiled=True)
    frame_all = lax.all_gather(frames[0], "seq", axis=0, tiled=True)
    end = lax.broadcasted_iota(jnp.int32, (1, length), 1) + 1
    padded = jnp.concatenate([frame_all, jnp.full((TAIL,), -1, jnp.int32)])
    for shift in range(1, TAIL):
        end = end + (padded[shift : shift + length] == frame_all).astype(jnp.int32)[None]

    cot = cotangent[0]
    grad_packed = call(
        grad_attention_kernel,
        "grad_attention",
        sds((group, half, 2 * HS), bf),
        (cot, weight),
        flops=2 * tok * width * width,
        nbytes=2 * width * width,
    )
    grad_heads = exchange(grad_packed, "seq")
    headbuf = pltpu.VMEM((length + TAIL, HS), bf)
    sumbuf = pltpu.VMEM((length + TAIL, HS), f32)
    o_packed, lse = call(
        fwd_kernel,
        "attention_forward",
        (sds((group, half, 2 * HS), bf), sds((1, length), f32)),
        (heads, end),
        (headbuf, headbuf, headbuf, pltpu.VMEM((2, HS, QH), f32), pltpu.VMEM((8, QH), f32)),
        flops=8 * length * length * HS // 2,
        nbytes=8 * length * HS,
    )
    o_tokens = exchange(o_packed, "seq")
    output, partial = call(
        output_kernel,
        "output_projection",
        (sds((tok, width), bf), sds((width, width), bf)),
        (o_tokens, weight, cot),
        (pltpu.VMEM((tok, width), bf),),
        flops=4 * tok * width * width,
        nbytes=4 * width * width,
    )
    grad_part = lax.psum_scatter(partial, "seq", scatter_dimension=0, tiled=True)
    grads = call(
        bwd_kernel,
        "attention_backward",
        sds((group, tok + half, 2 * HS), bf),
        (heads, grad_heads, o_packed, end, lse),
        (headbuf, headbuf, headbuf, pltpu.VMEM((2, HS, QH), f32), sumbuf, sumbuf),
        flops=20 * length * length * HS // 2,
        nbytes=16 * length * HS,
    )
    copies = jnp.broadcast_to(grad_part, (lax.axis_size("dp"), *grad_part.shape))
    grad_weight = exchange(copies, "dp").astype(f32).sum(axis=0)
    dq, dk, dv = call(
        unpack_qkv_kernel,
        "unpack_grads",
        (sds((tok, width), bf),) * 3,
        (exchange(grads, "seq"),),
        nbytes=6 * tok * width,
    )
    return output[None], dq[None], dk[None], dv[None], grad_weight


def solution(mesh):
    tokens = P("dp", "seq", None)
    return jax.shard_map(
        on_device,
        mesh=mesh,
        in_specs=(tokens, tokens, tokens, P("dp", "seq"), P("seq", None), tokens),
        out_specs=(tokens, tokens, tokens, tokens, P("seq", None)),
        check_vma=False,
    )
```

time: 488 us -> 372 us (0.76)
  blocking collectives: 34.2 us -> 190 us
  matrix products: 131 us -> 0 us
  Pallas kernels: 0 us -> 94.3 us
  local copies, waits for them, and re-layouts: 89.7 us -> 5.66 us
  other arithmetic: 66.4 us -> 2.92 us
  starting transfers between devices: 55.8 us -> 17.1 us
  waiting for transfers between devices: 70.4 us -> 47.2 us
  loops' own time: 22.7 us -> 0 us
    dot_general x297 -> x0, matrix products: 131 us -> none  [the longest x84 33.1 us: block_scores(): jnp.einsum('qhd,khd->hqk', query_rows, key_rows, preferred_element_type=j...]
    pallas_call x0 -> x6, Pallas kernels: none -> 94.3 us  [call(): pl.pallas_call(kernel, out_shape=outs, in_specs=[VM] * len(args), out_spe...]
    all_gather x0 -> x1, blocking collectives: none -> 85.3 us  [on_device(): frame_all = lax.all_gather(frames[0], 'seq', axis=0, tiled=True)]
    all_to_all x1 -> x3, blocking collectives: 34.2 us -> 104 us  [exchange(): return lax.all_to_all(array, axis, split_axis=0, concat_axis=0, tiled=True)]
    all_to_all x6 -> x2, waiting for transfers between devices: 69.1 us -> 23 us  [exchange(): return lax.all_to_all(array, axis, split_axis=0, concat_axis=0, tiled=True)]
    all_to_all x6 -> x2, starting transfers between devices: 55.5 us -> 17 us  [exchange(): return lax.all_to_all(array, axis, split_axis=0, concat_axis=0, tiled=True)]
    reduce_sum x59 -> x1, other arithmetic: 33.7 us -> 2.79 us  [on_device(): grad_weight = exchange(copies, 'dp').astype(f32).sum(axis=0)]
    unnamed x30 -> x10, local copies, waits for them, and re-layouts: 30.5 us -> 3.13 us
  transfers between devices with their start and end apart: 8 -> 4, of which waited for: 4 -> 2; matrix products, arithmetic and copies ran while one was open for 58% -> 0% of each run, Pallas kernels for 0% -> 23%
where the time goes in v1:
time: 372 us; the launch traced here: 371 us
  blocking collectives  190 us (51%)
  Pallas kernels  94.3 us (25%)
  waiting for transfers between devices  47.2 us (13%)
  starting transfers between devices  17.1 us (5%)
  between operations  14.1 us (4%)
  local copies, waits for them, and re-layouts  5.66 us (2%)
    all_to_all x3, blocking collectives, exchange(): return lax.all_to_all(array, axis, split_axis=0, concat_axis=0, tiled=True)  104 us
    pallas_call x6, Pallas kernels, call(): pl.pallas_call(kernel, out_shape=outs, in_specs=[VM] * len(args), out_spe...  94.3 us
    all_gather x1, blocking collectives, on_device(): frame_all = lax.all_gather(frames[0], 'seq', axis=0, tiled=True)  85.3 us
    reduce_scatter x1, waiting for transfers between devices, on_device(): lax.psum_scatter(partial, 'seq', scatter_dimension=0, tiled=True)  23.5 us
    all_to_all x2, waiting for transfers between devices, exchange(): return lax.all_to_all(array, axis, split_axis=0, concat_axis=0, tiled=True)  23 us
    all_to_all x2, starting transfers between devices, exchange(): return lax.all_to_all(array, axis, split_axis=0, concat_axis=0, tiled=True)  17 us
  transfers between devices with their start and end apart: 4, of which 2 were waited for; matrix products, arithmetic and copies ran while one was open for 0% of the time, Pallas kernels for 23%

profile of v1, /device:TPU:1, one launch (start us, length us, event | category | flops | bytes accessed | tf_op | source)
XLA Modules:
  0.0 370.9 jit_solution(5832096728715093758)
XLA Ops:
  7.2 0.0 all-gather.3.cloned.1.call-start
  7.2 0.7 all-gather.3.cloned.1.call-update
  7.9 0.0 copy-start.1
  7.9 1.0 copy-done.1
  8.9 0.0 copy-start.2
  8.9 1.0 copy-done.2
  10.0 0.0 copy-start.3
  10.0 1.0 copy-done.3
  11.0 2.1 pack_qkv.1
  13.1 0.0 copy-start.4
  13.1 12.7 %all-to-all-start = ((bf16[32,192,128]{2,1,0:T(8,128)(2,1)}), bf16[32,192,128]{2,1,0:T(8,128)(2,1)S(1)}, u32[]{:S(2)}, u32[]{:S(2)}) async-start(bf16[32,192,128]{2,1,0:T(8,128)(2,1)} %pack_qkv.1), calls=%async_computation | async-start | bytes 3145728 | tf_op jit(solution)/shard_map/all_to_all | solution.py:224
  25.8 0.0 reduce-scatter.2.cloned.1.call-start
  25.9 0.0 copy-done.4
  25.9 85.3 %all-gather = s32[1,4096]{1,0:T(1,128)S(1)} all-gather(s32[1,128]{1,0:T(1,128)S(1)} %copy-done.4), channel_id=2, replica_groups=mesh['dp'=8,'seq'=32] {'seq'}, dimensions={1}, use_global_device_ids=true | all-gather | bytes 16896 | tf_op jit(solution)/shard_map/all_gather | solution.py:243
  111.2 0.1 convert_add_fusion
  111.3 0.0 all-to-all-done.a_ref
  111.3 0.0 copy-start
  111.4 36.4 %attention_forward.1 = (bf16[32,64,128]{2,1,0:T(8,128)(2,1)S(1)}, f32[1,4096]{1,0:T(1,128)S(1)}) custom-call(bf16[32,192,128]{2,1,0:T(8,128)(2,1)S(1)} %all-to-all-done.a_ref, s32[1,4096]{1,0:T(1,128)S(1)} %bitcast.15), custom_call_target="tpu_custom_call" | custom-call | flops 4294967296 | bytes 2097152 | tf_op jit(solution)/shard_map/attention_forward/pallas_call | solution.py:211
  147.8 20.6 %all_to_all.25.o_ref = bf16[32,64,128]{2,1,0:T(8,128)(2,1)S(1)} all-to-all(bf16[32,64,128]{2,1,0:T(8,128)(2,1)S(1)} %get-tuple-element.12.o_ref), channel_id=1, replica_groups=mesh['dp'=8,'seq'=32] {'seq'}, dimensions={0} | all-to-all | bytes 1048576 | tf_op jit(solution)/shard_map/all_to_all | solution.py:224
  168.4 0.0 all-gather.3.cloned.1.call-done.w_ref
  168.4 0.0 copy-done
  168.4 10.2 %output_projection.1 = (bf16[128,2048]{1,0:T(8,128)(2,1)}, bf16[2048,2048]{1,0:T(8,128)(2,1)}) custom-call(bf16[32,64,128]{2,1,0:T(8,128)(2,1)S(1)} %all_to_all.25.o_ref, bf16[2048,2048]{1,0:T(8,128)(2,1)} %all-gather.3.cloned.1.call-done.w_ref, bf16[128,2048]{1,0:T(8,128)(2,1)S(1)} %bitcast.10), custom_call_target="tpu_custom_call" | custom-call | flops 2147483648 | bytes 16777216 | tf_op jit(solution)/shard_map/output_projection/pallas_call | solution.py:211
  178.7 0.0 reduce-scatter.2.cloned.1.call-update
  178.7 6.4 %grad_attention.1 = bf16[32,64,128]{2,1,0:T(8,128)(2,1)S(1)} custom-call(bf16[128,2048]{1,0:T(8,128)(2,1)S(1)} %bitcast.11, bf16[2048,2048]{1,0:T(8,128)(2,1)} %all-gather.3.cloned.1.call-done.w_ref), custom_call_target="tpu_custom_call" | custom-call | flops 1073741824 | bytes 8388608 | tf_op jit(solution)/shard_map/grad_attention/pallas_call | solution.py:211
  185.1 21.0 %all_to_all.26.do_ref = bf16[32,64,128]{2,1,0:T(8,128)(2,1)S(1)} all-to-all(bf16[32,64,128]{2,1,0:T(8,128)(2,1)S(1)} %grad_attention.1), channel_id=1, replica_groups=mesh['dp'=8,'seq'=32] {'seq'}, dimensions={0} | all-to-all | bytes 1048576 | tf_op jit(solution)/shard_map/all_to_all | solution.py:224
  206.1 37.1 %attention_backward.1 = bf16[32,192,128]{2,1,0:T(8,128)(2,1)S(1)} custom-call(bf16[32,192,128]{2,1,0:T(8,128)(2,1)S(1)} %all-to-all-done.a_ref, bf16[32,64,128]{2,1,0:T(8,128)(2,1)S(1)} %all_to_all.26.do_ref, bf16[32,64,128]{2,1,0:T(8,128)(2,1)S(1)} %get-tuple-element.12.o_ref, s32[1,4096]{1,0:T(1,128)S(1)} %bitcast.16, f32[1,4096]{1,0:T(1,128)S(1)} %get-tuple-element.14.lse_ref), custom_call_target="tpu_custom_call" | custom-call | flops 10737418240 | bytes 4194304 | tf_op jit(solution)/shard_map/attention_backward/pallas_call | solution.py:211
  243.2 62.6 %all_to_all.27.in_ref = bf16[32,192,128]{2,1,0:T(8,128)(2,1)S(1)} all-to-all(bf16[32,192,128]{2,1,0:T(8,128)(2,1)S(1)} %attention_backward.1), channel_id=1, replica_groups=mesh['dp'=8,'seq'=32] {'seq'}, dimensions={0} | all-to-all | bytes 3145728 | tf_op jit(solution)/shard_map/all_to_all | solution.py:224
  305.8 23.5 %reduce-scatter.2.cloned.1.call-done = bf16[64,2048]{1,0:T(8,128)(2,1)} async-done(((bf16[2048,2048]{1,0:T(8,128)(2,1)}), bf16[64,2048]{1,0:T(8,128)(2,1)}) %reduce-scatter.2.cloned.1.call-update) | async-done | bytes 262160 | tf_op jit(solution)/shard_map/reduce_scatter | solution.py:280
  329.3 2.5 broadcast_in_dim.14
  331.9 4.3 %all-to-all-start.4 = ((bf16[8,64,2048]{2,1,0:T(8,128)(2,1)}), bf16[8,64,2048]{2,1,0:T(8,128)(2,1)}, u32[]{:S(2)}, u32[]{:S(2)}) async-start(bf16[8,64,2048]{2,1,0:T(8,128)(2,1)} %broadcast_in_dim.14), calls=%async_computation.5 | async-start | bytes 4194304 | tf_op jit(solution)/shard_map/all_to_all | solution.py:224
  336.2 2.0 unpack_grads.1
  338.3 23.0 %all-to-all-done.4 = bf16[8,64,2048]{2,1,0:T(8,128)(2,1)} async-done(((bf16[8,64,2048]{2,1,0:T(8,128)(2,1)}), bf16[8,64,2048]{2,1,0:T(8,128)(2,1)}, u32[]{:S(2)}, u32[]{:S(2)}) %all-to-all-start.4) | async-done | bytes 2097184 | tf_op jit(solution)/shard_map/all_to_all | solution.py:224
  361.3 2.8 convert_reduce_fusion
Async XLA Ops:
  7.2 161.2 %all-gather.3.cloned.1.call-start = ((), (), s32[]{:S(2)}) async-start(), calls=%async_computation.6 | async-start | bytes 8650752 | tf_op jit(solution)/shard_map/all_gather | solution.py:242
  7.9 1.0 copy-start.1
  8.9 1.0 copy-start.2
  10.0 1.0 copy-start.3
  13.1 12.8 %copy-start.4 = (s32[1,128]{1,0:T(1,128)S(1)}, s32[1,128]{1,0:T(1,128)}, u32[]{:S(2)}) copy-start(s32[1,128]{1,0:T(1,128)} %param.9) | copy-start | bytes 1540
  13.1 98.2 %all-to-all-start = ((bf16[32,192,128]{2,1,0:T(8,128)(2,1)}), bf16[32,192,128]{2,1,0:T(8,128)(2,1)S(1)}, u32[]{:S(2)}, u32[]{:S(2)}) async-start(bf16[32,192,128]{2,1,0:T(8,128)(2,1)} %pack_qkv.1), calls=%async_computation | async-start | bytes 3145728 | tf_op jit(solution)/shard_map/all_to_all | solution.py:224
  25.8 303.5 %reduce-scatter.2.cloned.1.call-start = ((), (), s32[]{:S(2)}) async-start(), calls=%async_computation.7 | async-start | bytes 8650752 | tf_op jit(solution)/shard_map/reduce_scatter | solution.py:280
  111.3 57.1 %copy-start = (bf16[1,128,2048]{2,1,0:T(8,128)(2,1)S(1)}, bf16[1,128,2048]{2,1,0:T(8,128)(2,1)}, u32[]{:S(2)}) copy-start(bf16[1,128,2048]{2,1,0:T(8,128)(2,1)} %param.11) | copy-start | bytes 1572868
  331.9 29.4 %all-to-all-start.4 = ((bf16[8,64,2048]{2,1,0:T(8,128)(2,1)}), bf16[8,64,2048]{2,1,0:T(8,128)(2,1)}, u32[]{:S(2)}, u32[]{:S(2)}) async-start(bf16[8,64,2048]{2,1,0:T(8,128)(2,1)} %broadcast_in_dim.14), calls=%async_computation.5 | async-start | bytes 4194304 | tf_op jit(solution)/shard_map/all_to_all | solution.py:224
Sparse Core Ops, SparseCore 0:
  10.5 105.8 all-gather.2
  178.8 150.5 reduce-scatter.1

commit v2 on v1

--- a/solution.py
+++ b/solution.py
@@ -19,15 +19,23 @@
     return lax.dot_general(a, b, (((ca,), (cb,)), ((), ())), preferred_element_type=f32)
 
 
-def pack_qkv_kernel(q_ref, k_ref, v_ref, out_ref):
+def pack_qkv_kernel(q_ref, k_ref, v_ref, frame_ref, cot_ref, out_ref, cols_ref):
     tok = q_ref.shape[0]
     half = tok // 2
+    frame = frame_ref[...]
+    row = lax.broadcasted_iota(jnp.int32, (TAIL, tok), 0)
+    digits = jnp.where(row == 0, frame >> 4, jnp.where(row == 1, frame & 15, 0))
+    digits = digits.astype(f32).astype(bf)
+    part = cols_ref.shape[2]
+    for d in range(cols_ref.shape[0]):
+        cols_ref[d] = cot_ref[:, d * part : (d + 1) * part]
     for h in range(q_ref.shape[1] // HS):
         cols = slice(h * HS, (h + 1) * HS)
         out_ref[h, 0:tok, 0:HS] = q_ref[:, cols]
         out_ref[h, 0:tok, HS : 2 * HS] = k_ref[:, cols]
         out_ref[h, tok : tok + half, 0:HS] = v_ref[0:half, cols]
         out_ref[h, tok : tok + half, HS : 2 * HS] = v_ref[half:tok, cols]
+        out_ref[h, tok + half : tok + half + TAIL, :] = digits
 
 
 def unpack_qkv_kernel(in_ref, q_ref, k_ref, v_ref):
@@ -53,7 +61,7 @@
             out_ref[4 * c + i, :, HS : 2 * HS] = part[half:tok, cols]
 
 
-def output_kernel(o_ref, w_ref, cot_ref, out_ref, gw_ref, att):
+def output_kernel(o_ref, w_ref, out_ref, att):
     tok = out_ref.shape[0]
     half = tok // 2
     for h in range(o_ref.shape[0]):
@@ -64,13 +72,16 @@
     for c in range(width // 512):
         cols = slice(c * 512, (c + 1) * 512)
         out_ref[:, cols] = dg(att[...], w_ref[:, cols], 1, 0).astype(bf)
-    for c in range(att.shape[1] // 256):
+
+
+def weight_kernel(att_ref, cot_ref, gw_ref):
+    for c in range(att_ref.shape[1] // 256):
         rows = slice(c * 256, (c + 1) * 256)
-        gw_ref[rows, :] = dg(att[:, rows], cot_ref[...], 0, 0).astype(bf)
+        gw_ref[rows, :] = dg(att_ref[:, rows], cot_ref[...], 0, 0).astype(bf)
 
 
 def unpack_heads(a_ref, qp, kp, vp):
-    tok = 2 * a_ref.shape[1] // 3
+    tok = a_ref.shape[2]
     half = tok // 2
     length = a_ref.shape[0] * tok
     scale = jnp.asarray(HS**-0.5, bf)
@@ -88,9 +99,36 @@
     vp[length : length + TAIL, :] = jnp.zeros((TAIL, HS), bf)
 
 
-def fwd_kernel(a_ref, end_ref, o_ref, lse_ref, qp, kp, vp, acc, ml):
+def row_ends(a_ref, end_ref, fr):
+    tok = a_ref.shape[2]
+    half = tok // 2
+    blocks = a_ref.shape[0]
+
+    def load(t, c):
+        digits = a_ref[t, tok + half : tok + half + TAIL, :].astype(f32)
+        fr[0:1, pl.ds(pl.multiple_of(t * tok, tok), tok)] = digits[0:1, :] * 16.0 + digits[1:2, :]
+        return c
+
+    lax.fori_loop(0, blocks, load, 0)
+    fr[0:1, blocks * tok : (blocks + 1) * tok] = jnp.full((1, tok), -1.0, f32)
+
+    def count(t, c):
+        first = pl.multiple_of(t * tok, tok)
+        wide = fr[0:1, pl.ds(first, 2 * tok)]
+        own = wide[:, 0:tok]
+        end = lax.broadcasted_iota(jnp.int32, (1, tok), 1) + (first + 1)
+        for shift in range(1, TAIL):
+            end = end + (wide[:, shift : shift + tok] == own).astype(jnp.int32)
+        end_ref[0:1, pl.ds(first, tok)] = end
+        return c
+
+    lax.fori_loop(0, blocks, count, 0)
+
+
+def fwd_kernel(a_ref, o_ref, lse_ref, end_ref, qp, kp, vp, acc, ml, fr):
     unpack_heads(a_ref, qp, kp, vp)
-    tok = 2 * a_ref.shape[1] // 3
+    row_ends(a_ref, end_ref, fr)
+    tok = a_ref.shape[2]
     half = tok // 2
     length = a_ref.shape[0] * tok
 
@@ -140,7 +178,7 @@
 
 def bwd_kernel(a_ref, do_ref, o_ref, end_ref, lse_ref, g_ref, qp, kp, vp, dqa, dka, dva):
     unpack_heads(a_ref, qp, kp, vp)
-    tok = 2 * a_ref.shape[1] // 3
+    tok = a_ref.shape[2]
     half = tok // 2
     length = a_ref.shape[0] * tok
     dka[...] = jnp.zeros_like(dka)
@@ -231,22 +269,18 @@
     sds = jax.ShapeDtypeStruct
     half = tok // 2
 
-    packed = call(
+    clips = lax.axis_size("dp")
+    cot = cotangent[0]
+    packed, cot_cols = call(
         pack_qkv_kernel,
         "pack_qkv",
-        sds((group, tok + half, 2 * HS), bf),
-        (queries[0], keys[0], values[0]),
+        (sds((group, tok + half + TAIL, 2 * HS), bf), sds((clips, tok, width // clips), bf)),
+        (queries[0], keys[0], values[0], frames, cot),
         nbytes=6 * tok * width,
     )
     heads = exchange(packed, "seq")
     weight = lax.all_gather(out_weight, "seq", axis=0, tiled=True)
-    frame_all = lax.all_gather(frames[0], "seq", axis=0, tiled=True)
-    end = lax.broadcasted_iota(jnp.int32, (1, length), 1) + 1
-    padded = jnp.concatenate([frame_all, jnp.full((TAIL,), -1, jnp.int32)])
-    for shift in range(1, TAIL):
-        end = end + (padded[shift : shift + length] == frame_all).astype(jnp.int32)[None]
-
-    cot = cotangent[0]
+    cot_group = exchange(cot_cols, "dp").reshape(clips * tok, width // clips)
     grad_packed = call(
         grad_attention_kernel,
         "grad_attention",
@@ -258,26 +292,46 @@
     grad_heads = exchange(grad_packed, "seq")
     headbuf = pltpu.VMEM((length + TAIL, HS), bf)
     sumbuf = pltpu.VMEM((length + TAIL, HS), f32)
-    o_packed, lse = call(
+    o_packed, lse, end = call(
         fwd_kernel,
         "attention_forward",
-        (sds((group, half, 2 * HS), bf), sds((1, length), f32)),
-        (heads, end),
-        (headbuf, headbuf, headbuf, pltpu.VMEM((2, HS, QH), f32), pltpu.VMEM((8, QH), f32)),
+        (
+            sds((group, half, 2 * HS), bf),
+            sds((1, length), f32),
+            sds((1, length), jnp.int32),
+        ),
+        (heads,),
+        (
+            headbuf,
+            headbuf,
+            headbuf,
+            pltpu.VMEM((2, HS, QH), f32),
+            pltpu.VMEM((8, QH), f32),
+            pltpu.VMEM((1, length + tok), f32),
+        ),
         flops=8 * length * length * HS // 2,
         nbytes=8 * length * HS,
     )
     o_tokens = exchange(o_packed, "seq")
-    output, partial = call(
+    output, att = call(
         output_kernel,
         "output_projection",
-        (sds((tok, width), bf), sds((width, width), bf)),
-        (o_tokens, weight, cot),
-        (pltpu.VMEM((tok, width), bf),),
-        flops=4 * tok * width * width,
-        nbytes=4 * width * width,
+        (sds((tok, width), bf), sds((tok, width), bf)),
+        (o_tokens, weight),
+        flops=2 * tok * width * width,
+        nbytes=2 * width * width,
+    )
+    att_group = lax.all_gather(att, "dp", axis=0, tiled=True)
+    partial = call(
+        weight_kernel,
+        "weight_partial",
+        sds((width, width // clips), bf),
+        (att_group, cot_group),
+        flops=2 * tok * width * width,
+        nbytes=2 * width * tok * clips,
     )
     grad_part = lax.psum_scatter(partial, "seq", scatter_dimension=0, tiled=True)
+    grad_weight = lax.all_gather(grad_part, "dp", axis=1, tiled=True).astype(f32)
     grads = call(
         bwd_kernel,
         "attention_backward",
@@ -287,8 +341,6 @@
         flops=20 * length * length * HS // 2,
         nbytes=16 * length * HS,
     )
-    copies = jnp.broadcast_to(grad_part, (lax.axis_size("dp"), *grad_part.shape))
-    grad_weight = exchange(copies, "dp").astype(f32).sum(axis=0)
     dq, dk, dv = call(
         unpack_qkv_kernel,
         "unpack_grads",

time: 372 us -> 419 us (1.13); the launches traced: 371 us -> 411 us
  waiting for transfers between devices: 47.2 us -> 142 us
  blocking collectives: 190 us -> 137 us
  starting transfers between devices: 17.1 us -> 10.5 us
    reduce_scatter x1, waiting for transfers between devices: 23.5 us -> 87.2 us  [on_device(): lax.psum_scatter(partial, 'seq', scatter_dimension=0, tiled=True)]
    all_gather x1, blocking collectives: 85.3 us -> 23 us  [on_device(): lax.all_gather(grad_part, 'dp', axis=1, tiled=True).astype(f32)]
    all_gather x0 -> x1, waiting for transfers between devices: none -> 54.1 us  [on_device(): att_group = lax.all_gather(att, 'dp', axis=0, tiled=True)]
    all_to_all x2, waiting for transfers between devices: 23 us -> 0.01 us  [exchange(): return lax.all_to_all(array, axis, split_axis=0, concat_axis=0, tiled=True)]
    all_to_all x3, blocking collectives: 104 us -> 114 us  [exchange(): return lax.all_to_all(array, axis, split_axis=0, concat_axis=0, tiled=True)]
    all_to_all x2, starting transfers between devices: 17 us -> 10.4 us  [exchange(): return lax.all_to_all(array, axis, split_axis=0, concat_axis=0, tiled=True)]
    unnamed x10 -> x20, local copies, waits for them, and re-layouts: 3.13 us -> 9.61 us
    pallas_call x6 -> x7, Pallas kernels: 94.3 us -> 97.5 us  [call(): pl.pallas_call(kernel, out_shape=outs, in_specs=[VM] * len(args), out_spe...]
  transfers between devices with their start and end apart: 4 -> 5, of which waited for: 2 -> 2; matrix products, arithmetic and copies ran while one was open for 0% -> 0% of each run, Pallas kernels for 23% -> 22%
where the time goes in v2:
time: 419 us; the launch traced here: 411 us
  waiting for transfers between devices  142 us (34%)
  blocking collectives  137 us (33%)
  Pallas kernels  97.5 us (23%)
  between operations  13.8 us (3%)
  starting transfers between devices  10.5 us (3%)
  local copies, waits for them, and re-layouts  9.61 us (2%)
    all_to_all x3, blocking collectives, exchange(): return lax.all_to_all(array, axis, split_axis=0, concat_axis=0, tiled=True)  114 us
    pallas_call x7, Pallas kernels, call(): pl.pallas_call(kernel, out_shape=outs, in_specs=[VM] * len(args), out_spe...  97.5 us
    reduce_scatter x1, waiting for transfers between devices, on_device(): lax.psum_scatter(partial, 'seq', scatter_dimension=0, tiled=True)  87.2 us
    all_gather x1, waiting for transfers between devices, on_device(): att_group = lax.all_gather(att, 'dp', axis=0, tiled=True)  54.1 us
    all_gather x1, blocking collectives, on_device(): lax.all_gather(grad_part, 'dp', axis=1, tiled=True).astype(f32)  23 us
    all_to_all x2, starting transfers between devices, exchange(): return lax.all_to_all(array, axis, split_axis=0, concat_axis=0, tiled=True)  10.4 us
    unnamed x20, local copies, waits for them, and re-layouts  9.61 us
  transfers between devices with their start and end apart: 5, of which 2 were waited for; matrix products, arithmetic and copies ran while one was open for 0% of the time, Pallas kernels for 22%

profile of v2, /device:TPU:1, one launch (start us, length us, event | category | flops | bytes accessed | tf_op | source)
XLA Modules:
  0.0 411.5 jit_solution(12199108812625208108)
XLA Ops:
  7.2 0.0 all-gather.3.cloned.1.call-start
  7.2 0.7 all-gather.3.cloned.1.call-update
  7.9 0.0 all-gather.5.cloned.1.call-start
  7.9 0.0 copy-start.1
  8.0 1.0 copy-done.1
  9.0 0.0 copy-start.6
  9.0 1.0 copy-done.6
  10.0 0.0 copy-start.7
  10.0 1.0 copy-done.7
  11.1 0.0 copy-start.8
  11.1 1.0 copy-done.8
  12.1 0.0 copy-start.9
  12.1 0.7 copy-done.9
  12.8 1.6 pack_qkv.1
  14.4 62.0 %all_to_all.25.a_ref = bf16[32,208,128]{2,1,0:T(8,128)(2,1)S(1)} all-to-all(bf16[32,208,128]{2,1,0:T(8,128)(2,1)S(1)} %get-tuple-element.15), channel_id=1, replica_groups=mesh['dp'=8,'seq'=32] {'seq'}, dimensions={0} | all-to-all | bytes 3407872 | tf_op jit(solution)/shard_map/all_to_all | solution.py:262
  76.4 0.0 copy-start.3
  76.4 42.3 %attention_forward.1 = (bf16[32,64,128]{2,1,0:T(8,128)(2,1)S(1)}, f32[1,4096]{1,0:T(1,128)S(1)}, s32[1,4096]{1,0:T(1,128)S(1)}) custom-call(bf16[32,208,128]{2,1,0:T(8,128)(2,1)S(1)} %all_to_all.25.a_ref), custom_call_target="tpu_custom_call" | custom-call | flops 4294967296 | bytes 2097152 | tf_op jit(solution)/shard_map/attention_forward/pallas_call | solution.py:249
  118.7 0.0 copy-done.3
  118.7 24.0 %all_to_all.26.o_ref = bf16[32,64,128]{2,1,0:T(8,128)(2,1)S(1)} all-to-all(bf16[32,64,128]{2,1,0:T(8,128)(2,1)S(1)} %get-tuple-element.16.o_ref), channel_id=1, replica_groups=mesh['dp'=8,'seq'=32] {'seq'}, dimensions={0} | all-to-all | bytes 1048576 | tf_op jit(solution)/shard_map/all_to_all | solution.py:262
  142.8 0.0 copy-start.2
  142.8 0.0 all-gather.3.cloned.1.call-done.w_ref
  142.8 5.7 %output_projection.1 = (bf16[128,2048]{1,0:T(8,128)(2,1)}, bf16[128,2048]{1,0:T(8,128)(2,1)}) custom-call(bf16[32,64,128]{2,1,0:T(8,128)(2,1)S(1)} %all_to_all.26.o_ref, bf16[2048,2048]{1,0:T(8,128)(2,1)} %all-gather.3.cloned.1.call-done.w_ref), custom_call_target="tpu_custom_call" | custom-call | flops 1073741824 | bytes 8388608 | tf_op jit(solution)/shard_map/output_projection/pallas_call | solution.py:249
  148.5 0.0 all-gather.5.cloned.1.call-update
  148.5 0.0 copy-done.2
  148.5 6.4 %grad_attention.1 = bf16[32,64,128]{2,1,0:T(8,128)(2,1)S(1)} custom-call(bf16[128,2048]{1,0:T(8,128)(2,1)S(1)} %bitcast.10, bf16[2048,2048]{1,0:T(8,128)(2,1)} %all-gather.3.cloned.1.call-done.w_ref), custom_call_target="tpu_custom_call" | custom-call | flops 1073741824 | bytes 8388608 | tf_op jit(solution)/shard_map/grad_attention/pallas_call | solution.py:249
  154.9 28.2 %all_to_all.27.do_ref = bf16[32,64,128]{2,1,0:T(8,128)(2,1)S(1)} all-to-all(bf16[32,64,128]{2,1,0:T(8,128)(2,1)S(1)} %grad_attention.1), channel_id=1, replica_groups=mesh['dp'=8,'seq'=32] {'seq'}, dimensions={0} | all-to-all | bytes 1048576 | tf_op jit(solution)/shard_map/all_to_all | solution.py:262
  183.1 5.2 %all-to-all-start.4 = ((bf16[8,128,256]{2,1,0:T(8,128)(2,1)}), bf16[8,128,256]{2,1,0:T(8,128)(2,1)S(1)}, u32[]{:S(2)}, u32[]{:S(2)}) async-start(bf16[8,128,256]{2,1,0:T(8,128)(2,1)} %get-tuple-element.24), calls=%async_computation.4 | async-start | bytes 1048576 | tf_op jit(solution)/shard_map/all_to_all | solution.py:262
  188.3 0.0 copy-start.4
  188.3 1.4 copy-done.4
  189.7 37.1 %attention_backward.1 = bf16[32,192,128]{2,1,0:T(8,128)(2,1)S(1)} custom-call(bf16[32,208,128]{2,1,0:T(8,128)(2,1)S(1)} %copy-done.4, bf16[32,64,128]{2,1,0:T(8,128)(2,1)S(1)} %all_to_all.27.do_ref, bf16[32,64,128]{2,1,0:T(8,128)(2,1)S(1)} %get-tuple-element.16.o_ref, s32[1,4096]{1,0:T(1,128)S(1)} %get-tuple-element.18.end_ref, ...), custom_call_target="tpu_custom_call" | custom-call | flops 10737418240 | bytes 4194304 | tf_op jit(solution)/shard_map/attention_backward/pallas_call | solution.py:249
  226.8 0.0 copy-start.5
  226.9 1.2 copy-done.5
  228.0 0.0 all-to-all-done.4
  228.0 5.2 %all-to-all-start.3 = ((bf16[32,192,128]{2,1,0:T(8,128)(2,1)}), bf16[32,192,128]{2,1,0:T(8,128)(2,1)S(1)}, u32[]{:S(2)}, u32[]{:S(2)}) async-start(bf16[32,192,128]{2,1,0:T(8,128)(2,1)} %copy-done.5), calls=%async_computation.3 | async-start | bytes 3145728 | tf_op jit(solution)/shard_map/all_to_all | solution.py:262
  233.2 0.0 reduce-scatter.2.cloned.1.call-start
  233.3 54.1 %all-gather.5.cloned.1.call-done.att_ref = bf16[1024,2048]{1,0:T(8,128)(2,1)} async-done(((bf16[128,2048]{1,0:T(8,128)(2,1)}), bf16[1024,2048]{1,0:T(8,128)(2,1)}) %all-gather.5.cloned.1.call-update) | async-done | bytes 4194320 | tf_op jit(solution)/shard_map/all_gather | solution.py:324
  287.4 0.0 copy-start
  287.4 2.2 copy-done
  289.6 2.3 weight_partial.1
  291.9 0.0 reduce-scatter.2.cloned.1.call-update
  291.9 0.0 all-to-all-done.3.in_ref
  291.9 2.0 unpack_grads.1
  294.0 87.2 %reduce-scatter.2.cloned.1.call-done = bf16[64,256]{1,0:T(8,128)(2,1)} async-done(((bf16[2048,256]{1,0:T(8,128)(2,1)}), bf16[64,256]{1,0:T(8,128)(2,1)}) %reduce-scatter.2.cloned.1.call-update) | async-done | bytes 32784 | tf_op jit(solution)/shard_map/reduce_scatter | solution.py:333
  381.1 23.0 %all_gather.11 = bf16[64,2048]{1,0:T(8,128)(2,1)S(1)} all-gather(bf16[64,256]{1,0:T(8,128)(2,1)} %reduce-scatter.2.cloned.1.call-done), channel_id=1, replica_groups=mesh['dp'=8,'seq'=32] {'dp'}, dimensions={1}, use_global_device_ids=true | all-gather | bytes 294912 | tf_op jit(solution)/shard_map/all_gather | solution.py:334
  404.1 0.8 convert_element_type.3
Async XLA Ops:
  7.2 135.6 %all-gather.3.cloned.1.call-start = ((), (), s32[]{:S(2)}) async-start(), calls=%async_computation.6 | async-start | bytes 8650752 | tf_op jit(solution)/shard_map/all_gather | solution.py:282
  7.9 279.5 %all-gather.5.cloned.1.call-start = ((), (), s32[]{:S(2)}) async-start(), calls=%async_computation.7 | async-start | bytes 4718592 | tf_op jit(solution)/shard_map/all_gather | solution.py:324
  7.9 1.0 copy-start.1
  9.0 1.0 copy-start.6
  10.0 1.0 copy-start.7
  11.1 1.0 copy-start.8
  12.1 0.7 copy-start.9
  76.4 42.3 %copy-start.3 = (bf16[32,208,128]{2,1,0:T(8,128)(2,1)}, bf16[32,208,128]{2,1,0:T(8,128)(2,1)S(1)}, u32[]{:S(2)}) copy-start(bf16[32,208,128]{2,1,0:T(8,128)(2,1)S(1)} %all_to_all.25.a_ref) | copy-start | bytes 5111812
  142.8 5.7 %copy-start.2 = (bf16[1,128,2048]{2,1,0:T(8,128)(2,1)S(1)}, bf16[1,128,2048]{2,1,0:T(8,128)(2,1)}, u32[]{:S(2)}) copy-start(bf16[1,128,2048]{2,1,0:T(8,128)(2,1)} %param.11) | copy-start | bytes 1572868
  183.1 45.0 %all-to-all-start.4 = ((bf16[8,128,256]{2,1,0:T(8,128)(2,1)}), bf16[8,128,256]{2,1,0:T(8,128)(2,1)S(1)}, u32[]{:S(2)}, u32[]{:S(2)}) async-start(bf16[8,128,256]{2,1,0:T(8,128)(2,1)} %get-tuple-element.24), calls=%async_computation.4 | async-start | bytes 1048576 | tf_op jit(solution)/shard_map/all_to_all | solution.py:262
  188.3 1.5 copy-start.4
  226.8 1.2 copy-start.5
  228.0 63.9 %all-to-all-start.3 = ((bf16[32,192,128]{2,1,0:T(8,128)(2,1)}), bf16[32,192,128]{2,1,0:T(8,128)(2,1)S(1)}, u32[]{:S(2)}, u32[]{:S(2)}) async-start(bf16[32,192,128]{2,1,0:T(8,128)(2,1)} %copy-done.5), calls=%async_computation.3 | async-start | bytes 3145728 | tf_op jit(solution)/shard_map/all_to_all | solution.py:262
  233.2 147.9 %reduce-scatter.2.cloned.1.call-start = ((), (), s32[]{:S(2)}) async-start(), calls=%async_computation.8 | async-start | bytes 1081344 | tf_op jit(solution)/shard_map/reduce_scatter | solution.py:333
  287.4 2.2 copy-start
Sparse Core Ops, SparseCore 0:
  10.5 109.3 all-gather.2
  148.6 138.7 all-gather.4
  292.0 89.0 reduce-scatter.1

commit v3 on v1

v3 whole, which is shorter than its diff:
```python
import jax
import jax.numpy as jnp
from jax import lax
from jax.experimental import pallas as pl
from jax.experimental.pallas import tpu as pltpu
from jax.sharding import PartitionSpec as P

HS = 64
QB = 512
QH = 256
TAIL = 16
NEG = -1e30
NX, NY, NZH, NZL = 4, 4, 4, 2
f32, bf = jnp.float32, jnp.bfloat16
VM = pl.BlockSpec(memory_space=pltpu.VMEM)
MESH = pl.DeviceIdType.MESH


def dg(a, b, ca, cb):
    return lax.dot_general(a, b, (((ca,), (cb,)), ((), ())), preferred_element_type=f32)


def place():
    d, s = lax.axis_index("dp"), lax.axis_index("seq")
    return d, s


def remote(src, dst, send, recv, device):
    return pltpu.make_async_remote_copy(
        src_ref=src, dst_ref=dst, send_sem=send, recv_sem=recv, device_id=device, device_id_type=MESH
    )


def others(count, me, body):
    def one(i, c):
        body((me + i) % count)
        return c

    lax.fori_loop(1, count, one, 0)


def forward_kernel(
    q_ref, k_ref, v_ref, frame_ref, cot_ref,
    qp, kp, vp, end_ref, lse_ref, osend, orecv, cotg,
    send, recv, fr, acc, ml,
    qkv_s, qkv_r, o_s, o_r, c_s, c_r,
):
    d, me = place()
    y, zl = d // NZL, d % NZL
    tok = q_ref.shape[0]
    half = tok // 2
    blocks = send.shape[0]
    length = blocks * tok
    quarter = cotg.shape[1]

    barrier = pltpu.get_barrier_semaphore()

    def greet(t):
        pl.semaphore_signal(barrier, inc=1, device_id=(d, t), device_id_type=MESH)

    def greet_y(t):
        pl.semaphore_signal(barrier, inc=1, device_id=(t * NZL + zl, me), device_id_type=MESH)

    others(blocks, me, greet)
    others(NY, y, greet_y)

    frame = frame_ref[...]
    row = lax.broadcasted_iota(jnp.int32, (TAIL, tok), 0)
    digits = jnp.where(row == 0, frame >> 4, jnp.where(row == 1, frame & 15, 0))
    digits = digits.astype(f32).astype(bf)
    for h in range(blocks):
        cols = slice(h * HS, (h + 1) * HS)
        send[h, 0:tok, 0:HS] = q_ref[:, cols]
        send[h, 0:tok, HS : 2 * HS] = k_ref[:, cols]
        send[h, tok : tok + half, 0:HS] = v_ref[0:half, cols]
        send[h, tok : tok + half, HS : 2 * HS] = v_ref[half:tok, cols]
        send[h, tok + half : tok + half + TAIL, :] = digits
    pl.semaphore_wait(barrier, blocks - 1 + NY - 1)

    def qkv(t, src):
        return remote(send.at[t], recv.at[src], qkv_s.at[t], qkv_r.at[src], (d, t))

    def cot_copy(t, src):
        cols = pl.ds(pl.multiple_of(t * quarter, quarter), quarter)
        rows = pl.ds(pl.multiple_of(src * tok, tok), tok)
        return remote(
            cot_ref.at[:, cols], cotg.at[rows, :], c_s.at[t], c_r.at[src], (t * NZL + zl, me)
        )

    others(blocks, me, lambda t: qkv(t, me).start())
    others(NY, y, lambda t: cot_copy(t, y).start())
    recv[me] = send[me]
    cotg[pl.ds(pl.multiple_of(y * tok, tok), tok), :] = cot_ref[
        :, pl.ds(pl.multiple_of(y * quarter, quarter), quarter)
    ]
    others(blocks, me, lambda t: qkv(t, t).wait_recv())

    scale = jnp.asarray(HS**-0.5, bf)

    def unpack(t, c):
        first = pl.multiple_of(t * tok, tok)
        qp[pl.ds(first, tok), :] = recv[t, 0:tok, 0:HS] * scale
        kp[pl.ds(first, tok), :] = recv[t, 0:tok, HS : 2 * HS]
        vp[pl.ds(first, half), :] = recv[t, tok : tok + half, 0:HS]
        vp[pl.ds(first + half, half), :] = recv[t, tok : tok + half, HS : 2 * HS]
        dig = recv[t, tok + half : tok + half + TAIL, :].astype(f32)
        fr[0:1, pl.ds(first, tok)] = dig[0:1, :] * 16.0 + dig[1:2, :]
        return c

    lax.fori_loop(0, blocks, unpack, 0)
    kp[length : length + TAIL, :] = jnp.zeros((TAIL, HS), bf)
    vp[length : length + TAIL, :] = jnp.zeros((TAIL, HS), bf)
    fr[0:1, length : length + tok] = jnp.full((1, tok), -1.0, f32)

    def count(t, c):
        first = pl.multiple_of(t * tok, tok)
        wide = fr[0:1, pl.ds(first, 2 * tok)]
        own = wide[:, 0:tok]
        end = lax.broadcasted_iota(jnp.int32, (1, tok), 1) + (first + 1)
        for shift in range(1, TAIL):
            end = end + (wide[:, shift : shift + tok] == own).astype(jnp.int32)
        end_ref[0:1, pl.ds(first, tok)] = end
        return c

    lax.fori_loop(0, blocks, count, 0)

    def o_copy(t, src):
        return remote(osend.at[t], orecv.at[src], o_s.at[t], o_r.at[src], (d, t))

    def tile(qh, h, k0, n, end):
        s = dg(kp[pl.ds(k0, n), :], qh, 1, 1)
        if end is not None:
            pos = lax.broadcasted_iota(jnp.int32, (n, QH), 0) + k0
            s = jnp.where(pos < end, s, NEG)
        m = ml[2 * h : 2 * h + 1, :]
        mn = jnp.maximum(m, jnp.max(s, axis=0, keepdims=True))
        p = jnp.exp(s - mn)
        al = jnp.exp(m - mn)
        ml[2 * h : 2 * h + 1, :] = mn
        ml[2 * h + 1 : 2 * h + 2, :] = ml[2 * h + 1 : 2 * h + 2, :] * al + jnp.sum(
            p, axis=0, keepdims=True
        )
        acc[h] = acc[h] * al + dg(vp[pl.ds(k0, n), :], p.astype(bf), 0, 0)

    def qblock(i, c):
        b = (i + me) % (length // QB)
        qs = pl.multiple_of(b * QB, QB)
        qh = [qp[pl.ds(qs + h * QH, QH), :] for h in range(2)]
        for h in range(2):
            ml[2 * h : 2 * h + 1, :] = jnp.full((1, QH), NEG, f32)
            ml[2 * h + 1 : 2 * h + 2, :] = jnp.zeros((1, QH), f32)
            acc[h] = jnp.zeros((HS, QH), f32)

        def kb(j, c):
            for h in range(2):
                tile(qh[h], h, pl.multiple_of(j * QB, QB), QB, None)
            return c

        lax.fori_loop(0, b, kb, 0)
        for h in range(2):
            tile(qh[h], h, qs, (h + 1) * QH + TAIL, end_ref[0:1, pl.ds(qs + h * QH, QH)])
        for h in range(2):
            total = ml[2 * h + 1 : 2 * h + 2, :]
            o = (acc[h] / total).T.astype(bf)
            for n in range(QH // tok):
                t = (QB // tok) * b + (QH // tok) * h + n
                osend[t, :, 0:HS] = o[n * tok : n * tok + half, :]
                osend[t, :, HS : 2 * HS] = o[n * tok + half : (n + 1) * tok, :]

            lse_ref[0:1, pl.ds(qs + h * QH, QH)] = ml[2 * h : 2 * h + 1, :] + jnp.log(total)
        for n in range(QB // tok):
            t = (QB // tok) * b + n

            @pl.when(t != me)
            def _():
                o_copy(t, me).start()

            @pl.when(t == me)
            def _():
                orecv[t] = osend[t]

        return c

    lax.fori_loop(0, length // QB, qblock, 0)

    others(blocks, me, lambda t: o_copy(t, t).wait_recv())
    others(NY, y, lambda t: cot_copy(t, t).wait_recv())
    others(blocks, me, lambda t: o_copy(t, me).wait_send())
    others(blocks, me, lambda t: qkv(t, me).wait_send())
    others(NY, y, lambda t: cot_copy(t, y).wait_send())


def backward_kernel(
    qp, kp, vp, end_ref, lse_ref, own_o, tok_o, cotg, w_ref, cot_ref,
    out_ref, dq_ref, dk_ref, dv_ref, gw_ref,
    attg, dosend, dorecv, dop, dl, kvsend, kvrecv, dqsend, dqrecv, dqt, dka, dva,
    gwp, s1recv, s2send, s2recv, piece,
    do_s, do_r, kv_s, kv_r, dq_s, dq_r, a_s, a_r, g1_s, g1_r, g2_s, g2_r, g3_s, g3_r,
):
    d, me = place()
    y, zl = d // NZL, d % NZL
    x, zh, core = me // (2 * NZH), (me // 2) % NZH, me % 2
    tok = out_ref.shape[0]
    half = tok // 2
    blocks = dosend.shape[0]
    length = blocks * tok
    steps = length // QB
    xc, zz = x * 2 + core, zh * NZL + zl
    wide = cotg.shape[1]
    dps = NY * NZL

    barrier = pltpu.get_barrier_semaphore()

    def greet(dev):
        pl.semaphore_signal(barrier, inc=1, device_id=dev, device_id_type=MESH)

    others(blocks, me, lambda t: greet((d, t)))
    others(dps, d, lambda t: greet((t, me)))
    across = y * NZL + (1 - zl)
    others(NZH, zh, lambda t: greet((across, x * 2 * NZH + t * 2 + core)))

    def do_copy(t, src):
        return remote(dosend.at[t], dorecv.at[src], do_s.at[t], do_r.at[src], (d, t))

    def kv_copy(t, src):
        return remote(kvsend.at[t], kvrecv.at[src], kv_s.at[t], kv_r.at[src], (d, t))

    def dq_copy(t, src):
        return remote(dqsend.at[t], dqrecv.at[src], dq_s.at[t], dq_r.at[src], (d, t))

    def att_copy(t, src):
        mine = pl.ds(pl.multiple_of(y * tok, tok), tok)
        rows = pl.ds(pl.multiple_of(src * tok, tok), tok)
        return remote(attg.at[mine, :], attg.at[rows, :], a_s.at[t], a_r.at[src], (t * NZL + zl, me))

    def g1_copy(t, src):
        dev = (d, (t // 2) * 2 * NZH + zh * 2 + t % 2)
        return remote(gwp.at[t], s1recv.at[src], g1_s.at[t], g1_r.at[src], dev)

    def g2_copy(t, src):
        dev = (y * NZL + t % NZL, x * 2 * NZH + (t // NZL) * 2 + core)
        return remote(s2send.at[t], s2recv.at[src], g2_s.at[t], g2_r.at[src], dev)

    def g3_copy(t, src):
        rows = pl.ds(pl.multiple_of((src % NZL) * (HS // NZL), HS // NZL), HS // NZL)
        cols = pl.ds(pl.multiple_of((src // NZL) * wide, wide), wide)
        return remote(piece, gw_ref.at[rows, cols], g3_s.at[t], g3_r.at[src], (t, me))

    first = pl.ds(pl.multiple_of(y * tok, tok), tok)
    upper = pl.ds(pl.multiple_of(y * tok, tok), half)
    lower = pl.ds(pl.multiple_of(y * tok + half, half), half)
    for h in range(blocks):
        cols = slice(h * HS, (h + 1) * HS)
        attg[upper, cols] = tok_o[h, :, 0:HS]
        attg[lower, cols] = tok_o[h, :, HS : 2 * HS]
    pl.semaphore_wait(barrier, blocks - 1 + dps - 1 + NZH - 1)
    others(NY, y, lambda t: att_copy(t, y).start())

    def grad_heads(i, c):
        g = (i + me // 4) % (blocks // 4)
        rows = pl.ds(pl.multiple_of(g * 4 * HS, 4 * HS), 4 * HS)
        part = dg(cot_ref[...], w_ref[rows, :], 1, 1).astype(bf)
        for n in range(4):
            t = 4 * g + n
            cols = slice(n * HS, (n + 1) * HS)
            dosend[t, :, 0:HS] = part[0:half, cols]
            dosend[t, :, HS : 2 * HS] = part[half:tok, cols]
        for n in range(4):
            t = 4 * g + n

            @pl.when(t != me)
            def _():
                do_copy(t, me).start()

            @pl.when(t == me)
            def _():
                dorecv[t] = dosend[t]

        return c

    lax.fori_loop(0, blocks // 4, grad_heads, 0)

    def project(i, c):
        cols = pl.ds(pl.multiple_of(i * 512, 512), 512)
        out_ref[:, cols] = dg(attg[first, :], w_ref[:, cols], 1, 0).astype(bf)
        return c

    lax.fori_loop(0, out_ref.shape[1] // 512, project, 0)
    dqt[...] = jnp.zeros_like(dqt)
    others(blocks, me, lambda t: do_copy(t, t).wait_recv())

    def deltas(t, c):
        a = pl.multiple_of(t * tok, tok)
        up, lo = dorecv[t, :, 0:HS], dorecv[t, :, HS : 2 * HS]
        dop[pl.ds(a, half), :] = up
        dop[pl.ds(a + half, half), :] = lo
        prod = dorecv[t].astype(f32) * own_o[t].astype(f32)
        turned = prod.T
        both = [jnp.sum(turned[n * HS : (n + 1) * HS, :], axis=0, keepdims=True) for n in range(2)]
        dl[0:1, pl.ds(a, tok)] = jnp.concatenate(both, axis=1)
        return c

    lax.fori_loop(0, blocks, deltas, 0)

    def tile(k0, a, n, q0, width, masked):
        qr = pl.ds(q0, width)
        kr = pl.ds(k0 + a, n)
        kk, qh, do = kp[kr, :], qp[qr, :], dop[qr, :]
        p = jnp.exp(dg(kk, qh, 1, 1) - lse_ref[0:1, qr])
        if masked:
            pos = lax.broadcasted_iota(jnp.int32, (n, width), 0) + (k0 + a)
            p = jnp.where(pos < end_ref[0:1, qr], p, 0.0)
        dp = dg(vp[kr, :], do, 1, 1)
        dva[a : a + n, :] = dva[a : a + n, :] + dg(p.astype(bf), do, 1, 0)
        ds = (p * (dp - dl[0:1, qr])).astype(bf)
        dka[a : a + n, :] = dka[a : a + n, :] + dg(ds, qh, 1, 0)
        dqt[:, qr] = dqt[:, qr] + dg(kk, ds, 0, 0)

    def kblock(i, c):
        j = (i + me) % steps
        ks = pl.multiple_of(j * QB, QB)
        dka[...] = jnp.zeros_like(dka)
        dva[...] = jnp.zeros_like(dva)

        @pl.when(j > 0)
        def _():
            tile(ks, 0, TAIL, pl.multiple_of(ks - tok, tok), tok, True)

        tile(ks, 0, QH + TAIL, ks, QH, True)
        tile(ks, 0, QB, pl.multiple_of(ks + QH, QH), QH, True)

        def later(b, c):
            qs = pl.multiple_of(b * QB, QB)
            for h in range(2):
                tile(ks, 0, QB, pl.multiple_of(qs + h * QH, QH), QH, False)
            return c

        lax.fori_loop(j + 1, steps, later, 0)
        for n in range(QB // tok):
            t = (QB // tok) * j + n
            kvsend[t, :, 0:HS] = dka[n * tok : (n + 1) * tok, :].astype(bf)
            kvsend[t, :, HS : 2 * HS] = dva[n * tok : (n + 1) * tok, :].astype(bf)
        for n in range(QB // tok):
            t = (QB // tok) * j + n

            @pl.when(t != me)
            def _():
                kv_copy(t, me).start()

            @pl.when(t == me)
            def _():
                kvrecv[t] = kvsend[t]

        @pl.when(i == 2)
        def _():
            others(NY, y, lambda t: att_copy(t, t).wait_recv())
            for g in range(blocks // 4):
                part = dg(attg[:, g * 4 * HS : (g + 1) * 4 * HS], cotg[...], 0, 0).astype(bf)
                for n in range(4):
                    h = 4 * g + n
                    to = (h // (2 * NZH)) * 2 + h % 2
                    at = ((h // 2) % NZH) * HS
                    gwp[to, at : at + HS, :] = part[n * HS : (n + 1) * HS, :]
            others(2 * NX, xc, lambda t: g1_copy(t, xc).start())

        @pl.when(i == 5)
        def _():
            others(2 * NX, xc, lambda t: g1_copy(t, t).wait_recv())
            s1recv[xc] = gwp[xc]
            for n in range(NZH * NZL):
                rows = slice(n * (HS // NZL), (n + 1) * (HS // NZL))
                total = s1recv[0, rows, :].astype(f32)
                for m in range(1, 2 * NX):
                    total = total + s1recv[m, rows, :].astype(f32)
                s2send[n] = total.astype(bf)
            others(NZH * NZL, zz, lambda t: g2_copy(t, zz).start())

        return c

    lax.fori_loop(0, steps, kblock, 0)

    def queries_done(i, c):
        t = (i + me) % blocks
        a = pl.multiple_of(t * tok, tok)
        dq = (dqt[:, pl.ds(a, tok)] * (HS**-0.5)).T.astype(bf)
        dqsend[t, :, 0:HS] = dq[0:half, :]
        dqsend[t, :, HS : 2 * HS] = dq[half:tok, :]

        @pl.when(t != me)
        def _():
            dq_copy(t, me).start()

        @pl.when(t == me)
        def _():
            dqrecv[t] = dqsend[t]

        return c

    lax.fori_loop(0, blocks, queries_done, 0)

    others(NZH * NZL, zz, lambda t: g2_copy(t, t).wait_recv())
    s2recv[zz] = s2send[zz]
    total = s2recv[0].astype(f32)
    for m in range(1, NZH * NZL):
        total = total + s2recv[m].astype(f32)
    piece[...] = total
    others(dps, d, lambda t: g3_copy(t, d).start())
    gw_ref[
        pl.ds(pl.multiple_of(zl * (HS // NZL), HS // NZL), HS // NZL),
        pl.ds(pl.multiple_of(y * wide, wide), wide),
    ] = total

    others(blocks, me, lambda t: kv_copy(t, t).wait_recv())
    for h in range(blocks):
        cols = slice(h * HS, (h + 1) * HS)
        dk_ref[:, cols] = kvrecv[h, :, 0:HS]
        dv_ref[:, cols] = kvrecv[h, :, HS : 2 * HS]
    others(blocks, me, lambda t: dq_copy(t, t).wait_recv())
    for h in range(blocks):
        cols = slice(h * HS, (h + 1) * HS)
        dq_ref[0:half, cols] = dqrecv[h, :, 0:HS]
        dq_ref[half:tok, cols] = dqrecv[h, :, HS : 2 * HS]
    others(dps, d, lambda t: g3_copy(t, t).wait_recv())
    others(blocks, me, lambda t: do_copy(t, me).wait_send())
    others(blocks, me, lambda t: kv_copy(t, me).wait_send())
    others(blocks, me, lambda t: dq_copy(t, me).wait_send())
    others(NY, y, lambda t: att_copy(t, y).wait_send())
    others(2 * NX, xc, lambda t: g1_copy(t, xc).wait_send())
    others(NZH * NZL, zz, lambda t: g2_copy(t, zz).wait_send())
    others(dps, d, lambda t: g3_copy(t, d).wait_send())


def call(kernel, name, cid, outs, args, scratch, flops, nbytes):
    return pl.pallas_call(
        kernel,
        out_shape=outs,
        in_specs=[VM] * len(args),
        out_specs=jax.tree.map(lambda _: VM, outs),
        scratch_shapes=scratch,
        compiler_params=pltpu.CompilerParams(
            vmem_limit_bytes=56 << 20, collective_id=cid, has_side_effects=True
        ),
        cost_estimate=pl.CostEstimate(flops=flops, bytes_accessed=nbytes, transcendentals=0),
        name=name,
    )(*args)


def on_device(queries, keys, values, frames, out_weight, cotangent):
    tok, width = queries.shape[1], queries.shape[2]
    group = lax.axis_size("seq")
    length = tok * group
    half = tok // 2
    sds = jax.ShapeDtypeStruct
    vmem = pltpu.VMEM

    def sems(n):
        return [pltpu.SemaphoreType.DMA((n,))] * 2

    weight = lax.all_gather(out_weight, "seq", axis=0, tiled=True)
    cot = cotangent[0]
    packed = (group, half, 2 * HS)
    qp, kp, vp, end, lse, own_o, tok_o, cotg = call(
        forward_kernel,
        "attention_forward",
        0,
        (
            sds((length, HS), bf),
            sds((length + TAIL, HS), bf),
            sds((length + TAIL, HS), bf),
            sds((1, length), jnp.int32),
            sds((1, length), f32),
            sds(packed, bf),
            sds(packed, bf),
            sds((NY * tok, width // NY), bf),
        ),
        (queries[0], keys[0], values[0], frames, cot),
        [
            vmem((group, tok + half + TAIL, 2 * HS), bf),
            vmem((group, tok + half + TAIL, 2 * HS), bf),
            vmem((1, length + tok), f32),
            vmem((2, HS, QH), f32),
            vmem((8, QH), f32),
            *sems(group),
            *sems(group),
            *sems(NY),
        ],
        8 * length * length * HS,
        8 * length * HS,
    )
    output, dq, dk, dv, gw = call(
        backward_kernel,
        "attention_backward",
        1,
        (sds((tok, width), bf),) * 4 + (sds((HS, width), f32),),
        (qp, kp, vp, end, lse, own_o, tok_o, cotg, weight, cot),
        [
            vmem((NY * tok, width), bf),
            vmem(packed, bf),
            vmem(packed, bf),
            vmem((length, HS), bf),
            vmem((1, length), f32),
            vmem((group, tok, 2 * HS), bf),
            vmem((group, tok, 2 * HS), bf),
            vmem(packed, bf),
            vmem(packed, bf),
            vmem((HS, length), f32),
            vmem((QB, HS), f32),
            vmem((QB, HS), f32),
            vmem((2 * NX, NZH * HS, width // NY), bf),
            vmem((2 * NX, NZH * HS, width // NY), bf),
            vmem((NZH * NZL, HS // NZL, width // NY), bf),
            vmem((NZH * NZL, HS // NZL, width // NY), bf),
            vmem((HS // NZL, width // NY), f32),
            *sems(group),
            *sems(group),
            *sems(group),
            *sems(NY),
            *sems(2 * NX),
            *sems(NZH * NZL),
            *sems(NY * NZL),
        ],
        20 * length * length * HS,
        16 * length * HS,
    )
    return output[None], dq[None], dk[None], dv[None], gw


def solution(mesh):
    tokens = P("dp", "seq", None)
    return jax.shard_map(
        on_device,
        mesh=mesh,
        in_specs=(tokens, tokens, tokens, P("dp", "seq"), P("seq", None), tokens),
        out_specs=(tokens, tokens, tokens, tokens, P("seq", None)),
        check_vma=False,
    )
```

time: 372 us -> 245 us (0.66)
  blocking collectives: 190 us -> 0 us
  Pallas kernels: 94.3 us -> 223 us
  waiting for transfers between devices: 47.2 us -> 2.48 us
  starting transfers between devices: 17.1 us -> 0.04 us
    pallas_call x6 -> x2, Pallas kernels: 94.3 us -> 223 us  [call(): pl.pallas_call(kernel, out_shape=outs, in_specs=[VM] * len(args), out_spe...]
    all_to_all x3 -> x0, blocking collectives: 104 us -> none  [exchange(): return lax.all_to_all(array, axis, split_axis=0, concat_axis=0, tiled=True)]
    all_gather x1 -> x0, blocking collectives: 85.3 us -> none  [on_device(): frame_all = lax.all_gather(frames[0], 'seq', axis=0, tiled=True)]
    reduce_scatter x1 -> x0, waiting for transfers between devices: 23.5 us -> none  [on_device(): lax.psum_scatter(partial, 'seq', scatter_dimension=0, tiled=True)]
    all_to_all x2 -> x0, waiting for transfers between devices: 23 us -> none  [exchange(): return lax.all_to_all(array, axis, split_axis=0, concat_axis=0, tiled=True)]
    all_to_all x2 -> x0, starting transfers between devices: 17 us -> none  [exchange(): return lax.all_to_all(array, axis, split_axis=0, concat_axis=0, tiled=True)]
  transfers between devices with their start and end apart: 4 -> 1, of which waited for: 2 -> 1; matrix products, arithmetic and copies ran while one was open for 0% -> 0% of each run, Pallas kernels for 23% -> 45%
where the time goes in v3:
time: 245 us
  Pallas kernels  223 us (91%)
  between operations  14.1 us (6%)
  local copies, waits for them, and re-layouts  5.16 us (2%)
  waiting for transfers between devices  2.48 us (1%)
    pallas_call x2, Pallas kernels, call(): pl.pallas_call(kernel, out_shape=outs, in_specs=[VM] * len(args), out_spe...  223 us
    unnamed x13, local copies, waits for them, and re-layouts  5.16 us
  transfers between devices with their start and end apart: 1, of which 1 were waited for; matrix products, arithmetic and copies ran while one was open for 0% of the time, Pallas kernels for 45%

profile of v3, /device:TPU:1, one launch (start us, length us, event | category | flops | bytes accessed | tf_op | source)
XLA Modules:
  0.0 244.6 jit_solution(15949440581231033272)
XLA Ops:
  7.2 0.0 all-gather.2.cloned.1.call-start
  7.2 0.7 all-gather.2.cloned.1.call-update
  7.9 111.0 %attention_forward.1 = (bf16[4096,64]{1,0:T(8,128)(2,1)}, bf16[4112,64]{1,0:T(8,128)(2,1)}, bf16[4112,64]{1,0:T(8,128)(2,1)}, s32[1,4096]{1,0:T(1,128)}, f32[1,4...) custom-call(bf16[128,2048]{1,0:T(8,128)(2,1)} %bitcast.12, ...), custom_call_target="tpu_custom_call" | custom-call | flops 8589934592 | bytes 2097152 | tf_op jit(solution)/shard_map/attention_forward/pallas_call | solution.py:434
  118.9 1.8 all-gather.2.cloned.1.call-done.w_ref
  120.8 111.9 %attention_backward.1 = (bf16[128,2048]{1,0:T(8,128)(2,1)}, bf16[128,2048]{1,0:T(8,128)(2,1)}, bf16[128,2048]{1,0:T(8,128)(2,1)}, bf16[128,2048]{1,0:T(8,128)(2,1)}, f32[64,2048]{1,0:T(8,128)}) custom-call(bf16[4096,64]{1,0:T(8,128)(2,1)} %get-tuple-element.18.qp, bf16[4112,64]{1,0:T(8,128)(2,1)} %get-tuple-element.19.kp, ...), custom_call_target="tpu_custom_call" | custom-call | flops 21474836480 | bytes 4194304 | tf_op jit(solution)/shard_map/attention_backward/pallas_call | solution.py:434
  232.6 0.0 copy-start.3
  232.6 0.0 copy-start.2
  232.6 2.0 copy.16
  234.6 0.0 copy-done.3
  234.6 0.0 copy-start.1
  234.6 0.8 copy.17
  235.4 0.0 copy-done.2
  235.4 0.0 copy-start
  235.4 0.8 copy.18
  236.2 0.0 copy-done.1
  236.2 0.8 copy.19
  237.0 0.0 copy-done
  237.0 0.8 copy.20
Async XLA Ops:
  7.2 113.6 %all-gather.2.cloned.1.call-start = ((), (), s32[]{:S(2)}) async-start(), calls=%async_computation | async-start | bytes 8650752 | tf_op jit(solution)/shard_map/all_gather | solution.py:459
  232.6 2.0 copy-start.3
  232.6 2.8 %copy-start.2 = (bf16[128,2048]{1,0:T(8,128)(2,1)S(1)}, bf16[128,2048]{1,0:T(8,128)(2,1)}, u32[]{:S(2)}) copy-start(bf16[128,2048]{1,0:T(8,128)(2,1)} %get-tuple-element.28) | copy-start | bytes 1572868
  234.6 1.6 copy-start.1
  235.4 1.6 copy-start
Sparse Core Ops, SparseCore 0:
  10.5 110.1 all-gather.1

commit v4 on v3

v4 whole, which is shorter than its diff:
```python
import jax
import jax.numpy as jnp
from jax import lax
from jax.experimental import pallas as pl
from jax.experimental.pallas import tpu as pltpu
from jax.sharding import PartitionSpec as P

HS = 64
QB = 512
QH = 256
TAIL = 16
NEG = -1e30
NX, NY, NZH, NZL = 4, 4, 4, 2
f32, bf = jnp.float32, jnp.bfloat16
VM = pl.BlockSpec(memory_space=pltpu.VMEM)
MESH = pl.DeviceIdType.MESH


def dg(a, b, ca, cb):
    return lax.dot_general(a, b, (((ca,), (cb,)), ((), ())), preferred_element_type=f32)


def place():
    d, s = lax.axis_index("dp"), lax.axis_index("seq")
    return d, s


def remote(src, dst, send, recv, device):
    return pltpu.make_async_remote_copy(
        src_ref=src, dst_ref=dst, send_sem=send, recv_sem=recv, device_id=device, device_id_type=MESH
    )


def others(count, me, body):
    def one(i, c):
        body((me + i) % count)
        return c

    lax.fori_loop(1, count, one, 0)


def kernel(
    q_ref, k_ref, v_ref, frame_ref, cot_ref, w_ref,
    out_ref, dq_ref, dk_ref, dv_ref, gw_ref,
    send, recv, qp, kp, vp, fr, end_ref, lse_ref, acc, ml,
    wp, cotg, dysend, dyrecv, dosend, dot, ot, orecv, aysend, attp,
    kvsend, kvrecv, dqsend, dqrecv, dqt, dka, dva, dl,
    gwp, s1recv, s2send, s2recv, piece, psend, precv,
    qkv_s, qkv_r, do_s, do_r, o_s, o_r, kv_s, kv_r, dq_s, dq_r,
    c_s, c_r, dy_s, dy_r, ay_s, ay_r, p_s, p_r,
    w1_s, w1_r, w2_s, w2_r, w3_s, w3_r, g1_s, g1_r, g2_s, g2_r, g3_s, g3_r,
):
    d, me = place()
    y, zl = d // NZL, d % NZL
    x, zh, core = me // (2 * NZH), (me // 2) % NZH, me % 2
    xc, zz = x * 2 + core, zh * NZL + zl
    tok, width = q_ref.shape
    half = tok // 2
    blocks = send.shape[0]
    length = blocks * tok
    steps = length // QB
    per = HS // NY
    group = blocks // 2 * per
    dps = NY * NZL

    def seq_of(xx, zz_, cc):
        return xx * 2 * NZH + zz_ * 2 + cc

    def ydev(t):
        return (t * NZL + zl, me)

    def al(v, n):
        return pl.ds(pl.multiple_of(v * n, n), n)

    def row_of(h):
        return (h % 2) * group + (h // 2) * per

    barrier = pltpu.get_barrier_semaphore()

    def greet(dev):
        pl.semaphore_signal(barrier, inc=1, device_id=dev, device_id_type=MESH)

    others(blocks, me, lambda t: greet((d, t)))
    others(dps, d, lambda t: greet((t, me)))
    others(NZH, zh, lambda t: greet((y * NZL + (1 - zl), seq_of(x, t, core))))

    def qkv(t, src):
        return remote(send.at[t], recv.at[src], qkv_s.at[t], qkv_r.at[src], (d, t))

    def cot_copy(t, src):
        return remote(cot_ref, cotg.at[al(src, tok), :], c_s.at[t], c_r.at[src], ydev(t))

    def w1_copy(t, src):
        at = wp.at[core, pl.ds(pl.multiple_of((x * NZH + src) * per, per), per), :]
        return remote(w_ref.at[al(y, per), :], at, w1_s.at[t], w1_r.at[src], (d, seq_of(x, t, core)))

    def w2_copy(t, src):
        own = wp.at[core, al(x, NZH * per), :]
        at = wp.at[core, al(src, NZH * per), :]
        return remote(own, at, w2_s.at[t], w2_r.at[src], (d, seq_of(t, zh, core)))

    def w3_copy(c):
        return remote(wp.at[c], wp.at[c], w3_s.at[0], w3_r.at[0], (d, seq_of(x, zh, 1 - core)))

    def dy_copy(c, t, src):
        return remote(
            dysend.at[c, t], dyrecv.at[c, src], dy_s.at[c, t], dy_r.at[c, src], ydev(t)
        )

    def do_copy(t, src):
        return remote(dosend.at[t], dot.at[:, al(src, tok)], do_s.at[t], do_r.at[src], (d, t))

    def o_copy(t, src):
        return remote(ot.at[:, al(t, tok)], orecv.at[src], o_s.at[t], o_r.at[src], (d, t))

    def ay_copy(t, src):
        return remote(aysend.at[t], attp.at[:, al(src, tok)], ay_s.at[t], ay_r.at[src], ydev(t))

    def p_copy(t, src):
        return remote(psend.at[t], precv.at[src], p_s.at[t], p_r.at[src], ydev(t))

    def kv_copy(t, src):
        return remote(kvsend.at[t], kvrecv.at[src], kv_s.at[t], kv_r.at[src], (d, t))

    def dq_copy(t, src):
        return remote(dqsend.at[t], dqrecv.at[src], dq_s.at[t], dq_r.at[src], (d, t))

    def g1_copy(t, src):
        rows = pl.ds(pl.multiple_of((t % 2) * group + (t // 2) * NZH * per, NZH * per), NZH * per)
        dev = (d, seq_of(t // 2, zh, t % 2))
        return remote(gwp.at[rows, :], s1recv.at[src], g1_s.at[t], g1_r.at[src], dev)

    def g2_copy(t, src):
        dev = (y * NZL + t % NZL, seq_of(x, t // NZL, core))
        return remote(s2send.at[t], s2recv.at[src], g2_s.at[t], g2_r.at[src], dev)

    def g3_copy(t, src):
        return remote(piece, gw_ref.at[al(src, per // NZL), :], g3_s.at[t], g3_r.at[src], (t, me))

    frame = frame_ref[...]
    row = lax.broadcasted_iota(jnp.int32, (TAIL, tok), 0)
    digits = jnp.where(row == 0, frame >> 4, jnp.where(row == 1, frame & 15, 0))
    digits = digits.astype(f32).astype(bf)
    for h in range(blocks):
        cols = slice(h * HS, (h + 1) * HS)
        send[h, 0:tok, 0:HS] = q_ref[:, cols]
        send[h, 0:tok, HS : 2 * HS] = k_ref[:, cols]
        send[h, tok : tok + half, 0:HS] = v_ref[0:half, cols]
        send[h, tok : tok + half, HS : 2 * HS] = v_ref[half:tok, cols]
        send[h, tok + half : tok + half + TAIL, :] = digits
    pl.semaphore_wait(barrier, blocks - 1 + dps - 1 + NZH - 1)

    others(NZH, zh, lambda t: w1_copy(t, zh).start())
    others(NY, y, lambda t: cot_copy(t, y).start())
    wp[core, pl.ds(pl.multiple_of((x * NZH + zh) * per, per), per), :] = w_ref[al(y, per), :]
    cotg[al(y, tok), :] = cot_ref[...]
    recv[me] = send[me]

    def near(i, c):
        qkv((me + i) % (2 * NZH) + x * 2 * NZH, me).start()
        return c

    lax.fori_loop(1, 2 * NZH, near, 0)
    others(NZH, zh, lambda t: w1_copy(t, t).wait_recv())
    others(NX, x, lambda t: w2_copy(t, x).start())

    def far(i, c):
        qkv(((x + 1 + i // (2 * NZH)) % NX) * 2 * NZH + (me + i) % (2 * NZH), me).start()
        return c

    lax.fori_loop(0, (NX - 1) * 2 * NZH, far, 0)
    others(NX, x, lambda t: w2_copy(t, t).wait_recv())
    w3_copy(core).start()
    others(NY, y, lambda t: cot_copy(t, t).wait_recv())

    def grad_part(c):
        for b in range(NY):
            part = dg(wp[c], cotg[b * tok : (b + 1) * tok, :], 1, 1).astype(bf)
            dysend[c, b] = part
        others(NY, y, lambda t: dy_copy(c, t, y).start())
        dyrecv[c, y] = dysend[c, y]

    grad_part(core)
    w3_copy(1 - core).wait_recv()
    grad_part(1 - core)
    for c in range(2):
        others(NY, y, lambda t: dy_copy(c, t, t).wait_recv())

    def regroup(i, c):
        t = (me + i) % blocks
        rows = pl.ds(pl.multiple_of((t // 2) * per, per), per)
        for b in range(NY):
            dosend[t, b * per : (b + 1) * per, :] = dyrecv[t % 2, b, rows, :]

        @pl.when(t != me)
        def _():
            do_copy(t, me).start()

        @pl.when(t == me)
        def _():
            dot[:, al(t, tok)] = dosend[t]

        return c

    lax.fori_loop(0, blocks, regroup, 0)
    others(blocks, me, lambda t: qkv(t, t).wait_recv())

    scale = jnp.asarray(HS**-0.5, bf)

    def unpack(t, c):
        first = pl.multiple_of(t * tok, tok)
        qp[pl.ds(first, tok), :] = recv[t, 0:tok, 0:HS] * scale
        kp[pl.ds(first, tok), :] = recv[t, 0:tok, HS : 2 * HS]
        vp[pl.ds(first, half), :] = recv[t, tok : tok + half, 0:HS]
        vp[pl.ds(first + half, half), :] = recv[t, tok : tok + half, HS : 2 * HS]
        dig = recv[t, tok + half : tok + half + TAIL, :].astype(f32)
        fr[0:1, pl.ds(first, tok)] = dig[0:1, :] * 16.0 + dig[1:2, :]
        return c

    lax.fori_loop(0, blocks, unpack, 0)
    kp[length : length + TAIL, :] = jnp.zeros((TAIL, HS), bf)
    vp[length : length + TAIL, :] = jnp.zeros((TAIL, HS), bf)
    fr[0:1, length : length + tok] = jnp.full((1, tok), -1.0, f32)

    def count(t, c):
        first = pl.multiple_of(t * tok, tok)
        wide = fr[0:1, pl.ds(first, 2 * tok)]
        own = wide[:, 0:tok]
        end = lax.broadcasted_iota(jnp.int32, (1, tok), 1) + (first + 1)
        for shift in range(1, TAIL):
            end = end + (wide[:, shift : shift + tok] == own).astype(jnp.int32)
        end_ref[0:1, pl.ds(first, tok)] = end
        return c

    lax.fori_loop(0, blocks, count, 0)

    def score_tile(qh, h, k0, n, end):
        s = dg(kp[pl.ds(k0, n), :], qh, 1, 1)
        if end is not None:
            pos = lax.broadcasted_iota(jnp.int32, (n, QH), 0) + k0
            s = jnp.where(pos < end, s, NEG)
        m = ml[2 * h : 2 * h + 1, :]
        mn = jnp.maximum(m, jnp.max(s, axis=0, keepdims=True))
        p = jnp.exp(s - mn)
        alpha = jnp.exp(m - mn)
        ml[2 * h : 2 * h + 1, :] = mn
        ml[2 * h + 1 : 2 * h + 2, :] = ml[2 * h + 1 : 2 * h + 2, :] * alpha + jnp.sum(
            p, axis=0, keepdims=True
        )
        acc[h] = acc[h] * alpha + dg(vp[pl.ds(k0, n), :], p.astype(bf), 0, 0)

    def qblock(i, c):
        b = (i + me) % steps
        qs = pl.multiple_of(b * QB, QB)
        qh = [qp[pl.ds(qs + h * QH, QH), :] for h in range(2)]
        for h in range(2):
            ml[2 * h : 2 * h + 1, :] = jnp.full((1, QH), NEG, f32)
            ml[2 * h + 1 : 2 * h + 2, :] = jnp.zeros((1, QH), f32)
            acc[h] = jnp.zeros((HS, QH), f32)

        def kb(j, c):
            for h in range(2):
                score_tile(qh[h], h, pl.multiple_of(j * QB, QB), QB, None)
            return c

        lax.fori_loop(0, b, kb, 0)
        for h in range(2):
            score_tile(qh[h], h, qs, (h + 1) * QH + TAIL, end_ref[0:1, pl.ds(qs + h * QH, QH)])
        for h in range(2):
            total = ml[2 * h + 1 : 2 * h + 2, :]
            ot[:, pl.ds(qs + h * QH, QH)] = (acc[h] / total).astype(bf)
            lse_ref[0:1, pl.ds(qs + h * QH, QH)] = ml[2 * h : 2 * h + 1, :] + jnp.log(total)
        for n in range(QB // tok):
            t = (QB // tok) * b + n

            @pl.when(t != me)
            def _():
                o_copy(t, me).start()

            @pl.when(t == me)
            def _():
                orecv[t] = ot[:, al(t, tok)]

        return c

    lax.fori_loop(0, steps, qblock, 0)

    others(blocks, me, lambda t: do_copy(t, t).wait_recv())

    def deltas(t, c):
        cols = al(t, tok)
        prod = dot[:, cols].astype(f32) * ot[:, cols].astype(f32)
        dl[0:1, cols] = jnp.sum(prod, axis=0, keepdims=True)
        return c

    lax.fori_loop(0, blocks, deltas, 0)
    dqt[...] = jnp.zeros_like(dqt)
    others(blocks, me, lambda t: o_copy(t, t).wait_recv())
    for h in range(blocks):
        at = (h % 2) * group + (h // 2) * per
        for b in range(NY):
            aysend[b, at : at + per, :] = orecv[h, b * per : (b + 1) * per, :]
    others(NY, y, lambda t: ay_copy(t, y).start())
    attp[:, al(y, tok)] = aysend[y]

    def tile(k0, n, q0, size, masked):
        qr = pl.ds(q0, size)
        kr = pl.ds(k0, n)
        kk, qh, do = kp[kr, :], qp[qr, :], dot[:, qr]
        p = jnp.exp(dg(kk, qh, 1, 1) - lse_ref[0:1, qr])
        if masked:
            pos = lax.broadcasted_iota(jnp.int32, (n, size), 0) + k0
            p = jnp.where(pos < end_ref[0:1, qr], p, 0.0)
        dp = dg(vp[kr, :], do, 1, 0)
        dva[0:n, :] = dva[0:n, :] + dg(p.astype(bf), do, 1, 1)
        ds = (p * (dp - dl[0:1, qr])).astype(bf)
        dka[0:n, :] = dka[0:n, :] + dg(ds, qh, 1, 0)
        dqt[:, qr] = dqt[:, qr] + dg(kk, ds, 0, 0)

    def kblock(i, c):
        j = (i + me) % steps
        ks = pl.multiple_of(j * QB, QB)
        dka[...] = jnp.zeros_like(dka)
        dva[...] = jnp.zeros_like(dva)

        @pl.when(j > 0)
        def _():
            tile(ks, TAIL, pl.multiple_of(ks - tok, tok), tok, True)

        tile(ks, QH + TAIL, ks, QH, True)
        tile(ks, QB, pl.multiple_of(ks + QH, QH), QH, True)

        def later(b, c):
            qs = pl.multiple_of(b * QB, QB)
            for h in range(2):
                tile(ks, QB, pl.multiple_of(qs + h * QH, QH), QH, False)
            return c

        lax.fori_loop(j + 1, steps, later, 0)
        for n in range(QB // tok):
            t = (QB // tok) * j + n
            kvsend[t, :, 0:HS] = dka[n * tok : (n + 1) * tok, :].astype(bf)
            kvsend[t, :, HS : 2 * HS] = dva[n * tok : (n + 1) * tok, :].astype(bf)
        for n in range(QB // tok):
            t = (QB // tok) * j + n

            @pl.when(t != me)
            def _():
                kv_copy(t, me).start()

            @pl.when(t == me)
            def _():
                kvrecv[t] = kvsend[t]

        @pl.when(i == 1)
        def _():
            others(NY, y, lambda t: ay_copy(t, t).wait_recv())
            for g in range(width // 512):
                cols = slice(g * 512, (g + 1) * 512)
                gwp[:, cols] = dg(attp[...], cotg[:, cols], 1, 0).astype(bf)
            others(2 * NX, xc, lambda t: g1_copy(t, xc).start())

        @pl.when(i == 2)
        def _():
            for b in range(NY):
                mine = attp[:, b * tok : (b + 1) * tok].T
                part = dg(mine[:, 0:group], wp[0], 1, 0) + dg(mine[:, group : 2 * group], wp[1], 1, 0)
                psend[b] = part.astype(bf)
            others(NY, y, lambda t: p_copy(t, y).start())

        @pl.when(i == 5)
        def _():
            others(2 * NX, xc, lambda t: g1_copy(t, t).wait_recv())
            s1recv[xc] = gwp[
                pl.ds(pl.multiple_of(core * group + x * NZH * per, NZH * per), NZH * per), :
            ]
            size = per // NZL
            for n in range(NZH * NZL):
                total = s1recv[0, n * size : (n + 1) * size, :].astype(f32)
                for m in range(1, 2 * NX):
                    total = total + s1recv[m, n * size : (n + 1) * size, :].astype(f32)
                s2send[n] = total.astype(bf)
            others(NZH * NZL, zz, lambda t: g2_copy(t, zz).start())

        return c

    lax.fori_loop(0, steps, kblock, 0)

    def queries_done(i, c):
        t = (i + me) % blocks
        dq = (dqt[:, al(t, tok)] * (HS**-0.5)).T.astype(bf)
        dqsend[t, :, 0:HS] = dq[0:half, :]
        dqsend[t, :, HS : 2 * HS] = dq[half:tok, :]

        @pl.when(t != me)
        def _():
            dq_copy(t, me).start()

        @pl.when(t == me)
        def _():
            dqrecv[t] = dqsend[t]

        return c

    lax.fori_loop(0, blocks, queries_done, 0)

    others(NZH * NZL, zz, lambda t: g2_copy(t, t).wait_recv())
    s2recv[zz] = s2send[zz]
    total = s2recv[0].astype(f32)
    for m in range(1, NZH * NZL):
        total = total + s2recv[m].astype(f32)
    piece[...] = total
    others(dps, d, lambda t: g3_copy(t, d).start())
    gw_ref[al(d, per // NZL), :] = total

    others(NY, y, lambda t: p_copy(t, t).wait_recv())
    precv[y] = psend[y]
    for g in range(width // 512):
        cols = slice(g * 512, (g + 1) * 512)
        total = precv[0, :, cols].astype(f32)
        for b in range(1, NY):
            total = total + precv[b, :, cols].astype(f32)
        out_ref[:, cols] = total.astype(bf)

    others(blocks, me, lambda t: kv_copy(t, t).wait_recv())
    for h in range(blocks):
        cols = slice(h * HS, (h + 1) * HS)
        dk_ref[:, cols] = kvrecv[h, :, 0:HS]
        dv_ref[:, cols] = kvrecv[h, :, HS : 2 * HS]
    others(blocks, me, lambda t: dq_copy(t, t).wait_recv())
    for h in range(blocks):
        cols = slice(h * HS, (h + 1) * HS)
        dq_ref[0:half, cols] = dqrecv[h, :, 0:HS]
        dq_ref[half:tok, cols] = dqrecv[h, :, HS : 2 * HS]
    others(dps, d, lambda t: g3_copy(t, t).wait_recv())

    for mk in (qkv, do_copy, o_copy, kv_copy, dq_copy):
        others(blocks, me, lambda t: mk(t, me).wait_send())
    for mk in (cot_copy, ay_copy, p_copy):
        others(NY, y, lambda t: mk(t, y).wait_send())
    for c in range(2):
        others(NY, y, lambda t: dy_copy(c, t, y).wait_send())
    others(NZH, zh, lambda t: w1_copy(t, zh).wait_send())
    others(NX, x, lambda t: w2_copy(t, x).wait_send())
    w3_copy(core).wait_send()
    others(2 * NX, xc, lambda t: g1_copy(t, xc).wait_send())
    others(NZH * NZL, zz, lambda t: g2_copy(t, zz).wait_send())
    others(dps, d, lambda t: g3_copy(t, d).wait_send())


def on_device(queries, keys, values, frames, out_weight, cotangent):
    tok, width = queries.shape[1], queries.shape[2]
    group = lax.axis_size("seq")
    length = tok * group
    half = tok // 2
    sds = jax.ShapeDtypeStruct
    vmem = pltpu.VMEM
    per = HS // NY

    def sems(*n):
        return [pltpu.SemaphoreType.DMA(n)] * 2

    packed = (group, half, 2 * HS)
    args = (queries[0], keys[0], values[0], frames, cotangent[0], out_weight)
    output, dq, dk, dv, gw = pl.pallas_call(
        kernel,
        out_shape=(sds((tok, width), bf),) * 4 + (sds((HS, width), f32),),
        in_specs=[VM] * len(args),
        out_specs=(VM,) * 5,
        scratch_shapes=[
            vmem((group, tok + half + TAIL, 2 * HS), bf),
            vmem((group, tok + half + TAIL, 2 * HS), bf),
            vmem((length, HS), bf),
            vmem((length + TAIL, HS), bf),
            vmem((length + TAIL, HS), bf),
            vmem((1, length + tok), f32),
            vmem((1, length), jnp.int32),
            vmem((1, length), f32),
            vmem((2, HS, QH), f32),
            vmem((8, QH), f32),
            vmem((2, group // 2 * per, width), bf),
            vmem((NY * tok, width), bf),
            vmem((2, NY, group // 2 * per, tok), bf),
            vmem((2, NY, group // 2 * per, tok), bf),
            vmem((group, HS, tok), bf),
            vmem((HS, length), bf),
            vmem((HS, length), bf),
            vmem((group, HS, tok), bf),
            vmem((NY, group * per, tok), bf),
            vmem((group * per, NY * tok), bf),
            vmem((group, tok, 2 * HS), bf),
            vmem((group, tok, 2 * HS), bf),
            vmem(packed, bf),
            vmem(packed, bf),
            vmem((HS, length), f32),
            vmem((QB, HS), f32),
            vmem((QB, HS), f32),
            vmem((1, length), f32),
            vmem((group * per, width), bf),
            vmem((2 * NX, NZH * per, width), bf),
            vmem((NZH * NZL, per // NZL, width), bf),
            vmem((NZH * NZL, per // NZL, width), bf),
            vmem((per // NZL, width), f32),
            vmem((NY, tok, width), bf),
            vmem((NY, tok, width), bf),
            *sems(group),
            *sems(group),
            *sems(group),
            *sems(group),
            *sems(group),
            *sems(NY),
            *sems(2, NY),
            *sems(NY),
            *sems(NY),
            *sems(NZH),
            *sems(NX),
            *sems(1),
            *sems(2 * NX),
            *sems(NZH * NZL),
            *sems(NY * NZL),
        ],
        compiler_params=pltpu.CompilerParams(
            vmem_limit_bytes=60 << 20, collective_id=0, has_side_effects=True
        ),
        name="attention_step",
    )(*args)
    return output[None], dq[None], dk[None], dv[None], gw


def solution(mesh):
    tokens = P("dp", "seq", None)
    return jax.shard_map(
        on_device,
        mesh=mesh,
        in_specs=(tokens, tokens, tokens, P("dp", "seq"), P("seq", None), tokens),
        out_specs=(tokens, tokens, tokens, tokens, P("seq", None)),
        check_vma=False,
    )
```

time: 245 us -> 189 us (0.77)
  Pallas kernels: 223 us -> 182 us
  between operations: 14.1 us -> 0.65 us
  waiting for transfers between devices: 2.48 us -> 0 us
    pallas_call x2 -> x1, Pallas kernels: 223 us -> 182 us  [on_device(): pl.pallas_call(kernel, out_shape=(sds((tok, width), bf),) * 4 + (sds((HS,...]
  transfers between devices with their start and end apart: 1 -> 0, of which waited for: 1 -> 0; matrix products, arithmetic and copies ran while one was open for 0% -> 0% of each run, Pallas kernels for 45% -> 0%
where the time goes in v4:
time: 189 us
  Pallas kernels  182 us (96%)
  local copies, waits for them, and re-layouts  6.42 us (3%)
    pallas_call x1, Pallas kernels, on_device(): pl.pallas_call(kernel, out_shape=(sds((tok, width), bf),) * 4 + (sds((HS,...  182 us
    unnamed x13, local copies, waits for them, and re-layouts  6.42 us

profile of v4, /device:TPU:1, one launch (start us, length us, event | category | flops | bytes accessed | tf_op | source)
XLA Modules:
  0.0 189.2 jit_solution(4301881436980642165)
XLA Ops:
  0.6 182.1 %attention_step.1 = (bf16[128,2048]{1,0:T(8,128)(2,1)}, bf16[128,2048]{1,0:T(8,128)(2,1)}, bf16[128,2048]{1,0:T(8,128)(2,1)}, bf16[128,2048]{1,0:T(8,128)(2,1)}, f32[64,2048]{1,0:T(8,128)}) custom-call(bf16[128,2048]{1,0:T(8,128)(2,1)} %bitcast.8, bf16[128,2048]{1,0:T(8,128)(2,1)} %bitcast.9, bf16[128,2048]{1,0:T(8,128)(2,1)} %bitcast.10, ...), custom_call_target="tpu_custom_call" | custom-call | tf_op jit(solution)/shard_map/attention_step/pallas_call | solution.py:465
  182.7 0.0 copy-start.3
  182.7 1.9 %copy.16 = bf16[1,128,2048]{2,1,0:T(8,128)(2,1)} copy(bf16[1,128,2048]{2,1,0:T(8,128)(2,1)} %bitcast.15) | data formatting | bytes 1048576
  184.7 0.0 copy-done.3
  184.7 0.0 copy-start.2
  184.7 0.8 copy.17
  185.5 0.4 copy-done.2
  185.9 0.0 copy-start.1
  185.9 0.8 copy.18
  186.7 0.4 copy-done.1
  187.1 0.0 copy-start
  187.1 0.8 copy.19
  187.9 0.4 copy-done
  188.4 0.8 copy.20
Async XLA Ops:
  182.7 2.0 %copy-start.3 = (bf16[128,2048]{1,0:T(8,128)(2,1)S(1)}, bf16[128,2048]{1,0:T(8,128)(2,1)}, u32[]{:S(2)}) copy-start(bf16[128,2048]{1,0:T(8,128)(2,1)} %get-tuple-element.11) | copy-start | bytes 1572868
  184.7 1.2 copy-start.2
  185.9 1.2 copy-start.1
  187.1 1.2 copy-start

commit v5 on v4

--- a/solution.py
+++ b/solution.py
@@ -40,11 +40,12 @@
 
 
 def kernel(
-    q_ref, k_ref, v_ref, frame_ref, cot_ref, w_ref,
-    out_ref, dq_ref, dk_ref, dv_ref, gw_ref,
-    send, recv, qp, kp, vp, fr, end_ref, lse_ref, acc, ml,
+    q_hbm, k_hbm, v_hbm, frame_hbm, cot_hbm, w_hbm,
+    sum_ref, kvrecv, dqrecv, gw_ref,
+    q_ref, k_ref, v_ref, frame_ref, cot_ref, w_ref, in_s,
+    send, recv, qp, kp, vp, fr, end_ref, lse_ref, acc, mx, lx, sall,
     wp, cotg, dysend, dyrecv, dosend, dot, ot, orecv, aysend, attp,
-    kvsend, kvrecv, dqsend, dqrecv, dqt, dka, dva, dl,
+    kvsend, dqsend, dqt, dka, dva, dl,
     gwp, s1recv, s2send, s2recv, piece, psend, precv,
     qkv_s, qkv_r, do_s, do_r, o_s, o_r, kv_s, kv_r, dq_s, dq_r,
     c_s, c_r, dy_s, dy_r, ay_s, ay_r, p_s, p_r,
@@ -75,6 +76,21 @@
     def row_of(h):
         return (h % 2) * group + (h // 2) * per
 
+    inputs = [
+        pltpu.make_async_copy(a, b, in_s.at[n])
+        for n, (a, b) in enumerate(
+            (
+                (q_hbm, q_ref),
+                (k_hbm, k_ref),
+                (v_hbm, v_ref),
+                (frame_hbm, frame_ref),
+                (cot_hbm, cot_ref),
+                (w_hbm, w_ref),
+            )
+        )
+    ]
+    for copy in inputs:
+        copy.start()
     barrier = pltpu.get_barrier_semaphore()
 
     def greet(dev):
@@ -137,6 +153,8 @@
     def g3_copy(t, src):
         return remote(piece, gw_ref.at[al(src, per // NZL), :], g3_s.at[t], g3_r.at[src], (t, me))
 
+    for copy in inputs:
+        copy.wait()
     frame = frame_ref[...]
     row = lax.broadcasted_iota(jnp.int32, (TAIL, tok), 0)
     digits = jnp.where(row == 0, frame >> 4, jnp.where(row == 1, frame & 15, 0))
@@ -183,93 +201,119 @@
     grad_part(core)
     w3_copy(1 - core).wait_recv()
     grad_part(1 - core)
-    for c in range(2):
-        others(NY, y, lambda t: dy_copy(c, t, t).wait_recv())
-
-    def regroup(i, c):
-        t = (me + i) % blocks
-        rows = pl.ds(pl.multiple_of((t // 2) * per, per), per)
-        for b in range(NY):
-            dosend[t, b * per : (b + 1) * per, :] = dyrecv[t % 2, b, rows, :]
-
-        @pl.when(t != me)
-        def _():
-            do_copy(t, me).start()
-
-        @pl.when(t == me)
-        def _():
-            dot[:, al(t, tok)] = dosend[t]
-
-        return c
-
-    lax.fori_loop(0, blocks, regroup, 0)
-    others(blocks, me, lambda t: qkv(t, t).wait_recv())
-
     scale = jnp.asarray(HS**-0.5, bf)
 
-    def unpack(t, c):
+    def unpack(t):
         first = pl.multiple_of(t * tok, tok)
         qp[pl.ds(first, tok), :] = recv[t, 0:tok, 0:HS] * scale
         kp[pl.ds(first, tok), :] = recv[t, 0:tok, HS : 2 * HS]
         vp[pl.ds(first, half), :] = recv[t, tok : tok + half, 0:HS]
         vp[pl.ds(first + half, half), :] = recv[t, tok : tok + half, HS : 2 * HS]
         dig = recv[t, tok + half : tok + half + TAIL, :].astype(f32)
-        fr[0:1, pl.ds(first, tok)] = dig[0:1, :] * 16.0 + dig[1:2, :]
-        return c
-
-    lax.fori_loop(0, blocks, unpack, 0)
+        fr[pl.ds(t, 1), :] = dig[0:1, :] * 16.0 + dig[1:2, :]
+
+    def near_in(i, c):
+        t = (me + i) % (2 * NZH) + x * 2 * NZH
+        qkv(t, t).wait_recv()
+        unpack(t)
+        return c
+
+    def far_in(i, c):
+        t = ((x + NX - 1 - i // (2 * NZH)) % NX) * 2 * NZH + (me + i) % (2 * NZH)
+        qkv(t, t).wait_recv()
+        unpack(t)
+        return c
+
+    unpack(me)
+    lax.fori_loop(1, 2 * NZH, near_in, 0)
+    lax.fori_loop(0, (NX - 1) * 2 * NZH, far_in, 0)
     kp[length : length + TAIL, :] = jnp.zeros((TAIL, HS), bf)
     vp[length : length + TAIL, :] = jnp.zeros((TAIL, HS), bf)
-    fr[0:1, length : length + tok] = jnp.full((1, tok), -1.0, f32)
-
-    def count(t, c):
-        first = pl.multiple_of(t * tok, tok)
-        wide = fr[0:1, pl.ds(first, 2 * tok)]
-        own = wide[:, 0:tok]
-        end = lax.broadcasted_iota(jnp.int32, (1, tok), 1) + (first + 1)
-        for shift in range(1, TAIL):
-            end = end + (wide[:, shift : shift + tok] == own).astype(jnp.int32)
-        end_ref[0:1, pl.ds(first, tok)] = end
-        return c
-
-    lax.fori_loop(0, blocks, count, 0)
-
-    def score_tile(qh, h, k0, n, end):
-        s = dg(kp[pl.ds(k0, n), :], qh, 1, 1)
+    fr[blocks : blocks + 8, :] = jnp.full((8, tok), -1.0, f32)
+
+    own = fr[0:blocks, :]
+    wide = jnp.concatenate([own, fr[1 : blocks + 1, :]], axis=1)
+    end = lax.broadcasted_iota(jnp.int32, (blocks, tok), 1) + 1
+    end = end + lax.broadcasted_iota(jnp.int32, (blocks, tok), 0) * tok
+    for shift in range(1, TAIL):
+        end = end + (wide[:, shift : shift + tok] == own).astype(jnp.int32)
+    end_ref[...] = end
+
+    def ends(t, size):
+        return jnp.concatenate([end_ref[pl.ds(t + n, 1), :] for n in range(size // tok)], axis=1)
+
+    def fold(v, op):
+        return op(v.reshape(v.shape[0] // 8, 8, v.shape[1]), axis=0)
+
+    def stat(qh, h, k0, n, end):
+        sc = dg(kp[pl.ds(k0, n), :], qh, 1, 1)
         if end is not None:
             pos = lax.broadcasted_iota(jnp.int32, (n, QH), 0) + k0
-            s = jnp.where(pos < end, s, NEG)
-        m = ml[2 * h : 2 * h + 1, :]
-        mn = jnp.maximum(m, jnp.max(s, axis=0, keepdims=True))
-        p = jnp.exp(s - mn)
-        alpha = jnp.exp(m - mn)
-        ml[2 * h : 2 * h + 1, :] = mn
-        ml[2 * h + 1 : 2 * h + 2, :] = ml[2 * h + 1 : 2 * h + 2, :] * alpha + jnp.sum(
-            p, axis=0, keepdims=True
-        )
-        acc[h] = acc[h] * alpha + dg(vp[pl.ds(k0, n), :], p.astype(bf), 0, 0)
+            sc = jnp.where(pos < end, sc, NEG)
+        sall[h, pl.ds(k0, n), :] = sc
+        mx[h] = jnp.maximum(mx[h], fold(sc, jnp.max))
+
+    def gather(m, h, k0, n):
+        p = jnp.exp(sall[h, pl.ds(k0, n), :] - m)
+        lx[h] = lx[h] + fold(p, jnp.sum)
+        acc[h] = acc[h] + dg(vp[pl.ds(k0, n), :], p.astype(bf), 0, 0)
+
+    def in_pairs(first, last, body):
+        def two(j, c):
+            body(first + 2 * j)
+            body(first + 2 * j + 1)
+            return c
+
+        lax.fori_loop(0, (last - first) // 2, two, 0)
+
+        @pl.when((last - first) % 2 == 1)
+        def _():
+            body(last - 1)
+
+    def regroup(i, c):
+        t = (me + i) % blocks
+        rows = pl.ds(pl.multiple_of((t // 2) * per, per), per)
+        for b in range(NY):
+            dosend[t, b * per : (b + 1) * per, :] = dyrecv[t % 2, b, rows, :]
+
+        @pl.when(t != me)
+        def _():
+            do_copy(t, me).start()
+
+        @pl.when(t == me)
+        def _():
+            dot[:, al(t, tok)] = dosend[t]
+
+        return c
 
     def qblock(i, c):
         b = (i + me) % steps
         qs = pl.multiple_of(b * QB, QB)
         qh = [qp[pl.ds(qs + h * QH, QH), :] for h in range(2)]
+        mx[...] = jnp.full_like(mx, NEG)
+        lx[...] = jnp.zeros_like(lx)
+        acc[...] = jnp.zeros_like(acc)
         for h in range(2):
-            ml[2 * h : 2 * h + 1, :] = jnp.full((1, QH), NEG, f32)
-            ml[2 * h + 1 : 2 * h + 2, :] = jnp.zeros((1, QH), f32)
-            acc[h] = jnp.zeros((HS, QH), f32)
-
-        def kb(j, c):
+            stat(qh[h], h, qs, (h + 1) * QH + TAIL, ends((QB // tok) * b + (QH // tok) * h, QH))
+
+        def stats(j):
             for h in range(2):
-                score_tile(qh[h], h, pl.multiple_of(j * QB, QB), QB, None)
-            return c
-
-        lax.fori_loop(0, b, kb, 0)
+                stat(qh[h], h, pl.multiple_of(j * QB, QB), QB, None)
+
+        in_pairs(0, b, stats)
+        m = [jnp.max(mx[h], axis=0, keepdims=True) for h in range(2)]
         for h in range(2):
-            score_tile(qh[h], h, qs, (h + 1) * QH + TAIL, end_ref[0:1, pl.ds(qs + h * QH, QH)])
+            gather(m[h], h, qs, (h + 1) * QH + TAIL)
+
+        def gathers(j):
+            for h in range(2):
+                gather(m[h], h, pl.multiple_of(j * QB, QB), QB)
+
+        in_pairs(0, b, gathers)
         for h in range(2):
-            total = ml[2 * h + 1 : 2 * h + 2, :]
+            total = jnp.sum(lx[h], axis=0, keepdims=True)
             ot[:, pl.ds(qs + h * QH, QH)] = (acc[h] / total).astype(bf)
-            lse_ref[0:1, pl.ds(qs + h * QH, QH)] = ml[2 * h : 2 * h + 1, :] + jnp.log(total)
+            lse_ref[0:1, pl.ds(qs + h * QH, QH)] = m[h] + jnp.log(total)
         for n in range(QB // tok):
             t = (QB // tok) * b + n
 
@@ -280,6 +324,12 @@
             @pl.when(t == me)
             def _():
                 orecv[t] = ot[:, al(t, tok)]
+
+        @pl.when(i == 0)
+        def _():
+            for c in range(2):
+                others(NY, y, lambda t: dy_copy(c, t, t).wait_recv())
+            lax.fori_loop(0, blocks, regroup, 0)
 
         return c
 
@@ -295,22 +345,15 @@
 
     lax.fori_loop(0, blocks, deltas, 0)
     dqt[...] = jnp.zeros_like(dqt)
-    others(blocks, me, lambda t: o_copy(t, t).wait_recv())
-    for h in range(blocks):
-        at = (h % 2) * group + (h // 2) * per
-        for b in range(NY):
-            aysend[b, at : at + per, :] = orecv[h, b * per : (b + 1) * per, :]
-    others(NY, y, lambda t: ay_copy(t, y).start())
-    attp[:, al(y, tok)] = aysend[y]
-
-    def tile(k0, n, q0, size, masked):
+
+    def tile(k0, n, q0, size, end):
         qr = pl.ds(q0, size)
         kr = pl.ds(k0, n)
         kk, qh, do = kp[kr, :], qp[qr, :], dot[:, qr]
         p = jnp.exp(dg(kk, qh, 1, 1) - lse_ref[0:1, qr])
-        if masked:
+        if end is not None:
             pos = lax.broadcasted_iota(jnp.int32, (n, size), 0) + k0
-            p = jnp.where(pos < end_ref[0:1, qr], p, 0.0)
+            p = jnp.where(pos < end, p, 0.0)
         dp = dg(vp[kr, :], do, 1, 0)
         dva[0:n, :] = dva[0:n, :] + dg(p.astype(bf), do, 1, 1)
         ds = (p * (dp - dl[0:1, qr])).astype(bf)
@@ -320,23 +363,23 @@
     def kblock(i, c):
         j = (i + me) % steps
         ks = pl.multiple_of(j * QB, QB)
+        first = (QB // tok) * j
         dka[...] = jnp.zeros_like(dka)
         dva[...] = jnp.zeros_like(dva)
 
         @pl.when(j > 0)
         def _():
-            tile(ks, TAIL, pl.multiple_of(ks - tok, tok), tok, True)
-
-        tile(ks, QH + TAIL, ks, QH, True)
-        tile(ks, QB, pl.multiple_of(ks + QH, QH), QH, True)
-
-        def later(b, c):
+            tile(ks, TAIL, pl.multiple_of(ks - tok, tok), tok, ends(first - 1, tok))
+
+        tile(ks, QH + TAIL, ks, QH, ends(first, QH))
+        tile(ks, QB, pl.multiple_of(ks + QH, QH), QH, ends(first + QH // tok, QH))
+
+        def later(b):
             qs = pl.multiple_of(b * QB, QB)
             for h in range(2):
-                tile(ks, QB, pl.multiple_of(qs + h * QH, QH), QH, False)
-            return c
-
-        lax.fori_loop(j + 1, steps, later, 0)
+                tile(ks, QB, pl.multiple_of(qs + h * QH, QH), QH, None)
+
+        in_pairs(j + 1, steps, later)
         for n in range(QB // tok):
             t = (QB // tok) * j + n
             kvsend[t, :, 0:HS] = dka[n * tok : (n + 1) * tok, :].astype(bf)
@@ -351,6 +394,16 @@
             @pl.when(t == me)
             def _():
                 kvrecv[t] = kvsend[t]
+
+        @pl.when(i == 0)
+        def _():
+            others(blocks, me, lambda t: o_copy(t, t).wait_recv())
+            for h in range(blocks):
+                at = (h % 2) * group + (h // 2) * per
+                for b in range(NY):
+                    aysend[b, at : at + per, :] = orecv[h, b * per : (b + 1) * per, :]
+            others(NY, y, lambda t: ay_copy(t, y).start())
+            attp[:, al(y, tok)] = aysend[y]
 
         @pl.when(i == 1)
         def _():
@@ -420,18 +473,9 @@
         total = precv[0, :, cols].astype(f32)
         for b in range(1, NY):
             total = total + precv[b, :, cols].astype(f32)
-        out_ref[:, cols] = total.astype(bf)
-
+        sum_ref[:, cols] = total.astype(bf)
     others(blocks, me, lambda t: kv_copy(t, t).wait_recv())
-    for h in range(blocks):
-        cols = slice(h * HS, (h + 1) * HS)
-        dk_ref[:, cols] = kvrecv[h, :, 0:HS]
-        dv_ref[:, cols] = kvrecv[h, :, HS : 2 * HS]
     others(blocks, me, lambda t: dq_copy(t, t).wait_recv())
-    for h in range(blocks):
-        cols = slice(h * HS, (h + 1) * HS)
-        dq_ref[0:half, cols] = dqrecv[h, :, 0:HS]
-        dq_ref[half:tok, cols] = dqrecv[h, :, HS : 2 * HS]
     others(dps, d, lambda t: g3_copy(t, t).wait_recv())
 
     for mk in (qkv, do_copy, o_copy, kv_copy, dq_copy):
@@ -448,6 +492,19 @@
     others(dps, d, lambda t: g3_copy(t, d).wait_send())
 
 
+def finish_kernel(out_in, kvrecv, dqrecv, gw_in, out_ref, dq_ref, dk_ref, dv_ref, gw_ref):
+    tok, width = out_ref.shape
+    half = tok // 2
+    gw_ref[...] = gw_in[...]
+    out_ref[...] = out_in[...]
+    for h in range(kvrecv.shape[0]):
+        cols = slice(h * HS, (h + 1) * HS)
+        dk_ref[:, cols] = kvrecv[h, :, 0:HS]
+        dv_ref[:, cols] = kvrecv[h, :, HS : 2 * HS]
+        dq_ref[0:half, cols] = dqrecv[h, :, 0:HS]
+        dq_ref[half:tok, cols] = dqrecv[h, :, HS : 2 * HS]
+
+
 def on_device(queries, keys, values, frames, out_weight, cotangent):
     tok, width = queries.shape[1], queries.shape[2]
     group = lax.axis_size("seq")
@@ -462,22 +519,36 @@
 
     packed = (group, half, 2 * HS)
     args = (queries[0], keys[0], values[0], frames, cotangent[0], out_weight)
-    output, dq, dk, dv, gw = pl.pallas_call(
+    received = pl.pallas_call(
         kernel,
-        out_shape=(sds((tok, width), bf),) * 4 + (sds((HS, width), f32),),
-        in_specs=[VM] * len(args),
-        out_specs=(VM,) * 5,
+        out_shape=(
+            sds((tok, width), bf),
+            sds((group, tok, 2 * HS), bf),
+            sds(packed, bf),
+            sds((HS, width), f32),
+        ),
+        in_specs=[pl.BlockSpec(memory_space=pltpu.HBM)] * len(args),
+        out_specs=(VM,) * 4,
         scratch_shapes=[
+            vmem((tok, width), bf),
+            vmem((tok, width), bf),
+            vmem((tok, width), bf),
+            vmem((1, tok), jnp.int32),
+            vmem((tok, width), bf),
+            vmem((HS, width), bf),
+            pltpu.SemaphoreType.DMA((6,)),
             vmem((group, tok + half + TAIL, 2 * HS), bf),
             vmem((group, tok + half + TAIL, 2 * HS), bf),
             vmem((length, HS), bf),
             vmem((length + TAIL, HS), bf),
             vmem((length + TAIL, HS), bf),
-            vmem((1, length + tok), f32),
-            vmem((1, length), jnp.int32),
+            vmem((group + 8, tok), f32),
+            vmem((group, tok), jnp.int32),
             vmem((1, length), f32),
             vmem((2, HS, QH), f32),
-            vmem((8, QH), f32),
+            vmem((2, 8, QH), f32),
+            vmem((2, 8, QH), f32),
+            vmem((2, length + TAIL, QH), f32),
             vmem((2, group // 2 * per, width), bf),
             vmem((NY * tok, width), bf),
             vmem((2, NY, group // 2 * per, tok), bf),
@@ -489,8 +560,6 @@
             vmem((NY, group * per, tok), bf),
             vmem((group * per, NY * tok), bf),
             vmem((group, tok, 2 * HS), bf),
-            vmem((group, tok, 2 * HS), bf),
-            vmem(packed, bf),
             vmem(packed, bf),
             vmem((HS, length), f32),
             vmem((QB, HS), f32),
@@ -520,10 +589,18 @@
             *sems(NY * NZL),
         ],
         compiler_params=pltpu.CompilerParams(
-            vmem_limit_bytes=60 << 20, collective_id=0, has_side_effects=True
+            vmem_limit_bytes=59 << 20, collective_id=0, has_side_effects=True
         ),
         name="attention_step",
     )(*args)
+    output, dq, dk, dv, gw = pl.pallas_call(
+        finish_kernel,
+        out_shape=(sds((tok, width), bf),) * 4 + (sds((HS, width), f32),),
+        in_specs=[VM] * 4,
+        out_specs=(VM,) * 5,
+        compiler_params=pltpu.CompilerParams(vmem_limit_bytes=60 << 20),
+        name="finish",
+    )(*received)
     return output[None], dq[None], dk[None], dv[None], gw
 
 

time: 189 us -> 167 us (0.88)
  Pallas kernels: 182 us -> 166 us
  local copies, waits for them, and re-layouts: 6.42 us -> 0 us
    pallas_call x1 -> x2, Pallas kernels: 182 us -> 166 us  [the longest x1 162 us: on_device(): pl.pallas_call(kernel, out_shape=(sds((tok, width), bf), sds((group, tok,...]
    unnamed x13 -> x0, local copies, waits for them, and re-layouts: 6.42 us -> none
where the time goes in v5:
time: 167 us; the launch traced here: 166 us
  Pallas kernels  166 us (99%)
    pallas_call x1, Pallas kernels, on_device(): pl.pallas_call(kernel, out_shape=(sds((tok, width), bf), sds((group, tok,...  162 us
    pallas_call x1, Pallas kernels, on_device(): pl.pallas_call(finish_kernel, out_shape=(sds((tok, width), bf),) * 4 + (s...  4.05 us

profile of v5, /device:TPU:1, one launch (start us, length us, event | category | flops | bytes accessed | tf_op | source)
XLA Modules:
  0.0 166.4 jit_solution(18430312128318074131)
XLA Ops:
  0.6 161.7 %attention_step.1 = (bf16[128,2048]{1,0:T(8,128)(2,1)}, bf16[32,128,128]{2,1,0:T(8,128)(2,1)}, bf16[32,64,128]{2,1,0:T(8,128)(2,1)}, f32[64,2048]{1,0:T(8,128)}) custom-call(bf16[128,2048]{1,0:T(8,128)(2,1)} %bitcast.8, bf16[128,2048]{1,0:T(8,128)(2,1)} %bitcast.9, bf16[128,2048]{1,0:T(8,128)(2,1)} %bitcast.10, s32[1,128]{1,0:T(1,128)} %frame_hbm.1, ...), custom_call_target="tpu_custom_call" | custom-call | tf_op jit(solution)/shard_map/attention_step/pallas_call | solution.py:522
  162.3 4.1 %finish.1 = (bf16[128,2048]{1,0:T(8,128)(2,1)}, bf16[128,2048]{1,0:T(8,128)(2,1)}, bf16[128,2048]{1,0:T(8,128)(2,1)}, bf16[128,2048]{1,0:T(8,128)(2,1)}, f32[64,2048]{1,0:T(8,128)}) custom-call(bf16[128,2048]{1,0:T(8,128)(2,1)} %get-tuple-element.14.out_in, bf16[32,128,128]{2,1,0:T(8,128)(2,1)} %get-tuple-element.15.kvrecv, ...), custom_call_target="tpu_custom_call" | custom-call | tf_op jit(solution)/shard_map/finish/pallas_call | solution.py:596

commit v6 on v5

--- a/solution.py
+++ b/solution.py
@@ -46,15 +46,15 @@
     send, recv, qp, kp, vp, fr, end_ref, lse_ref, acc, mx, lx, sall,
     wp, cotg, dysend, dyrecv, dosend, dot, ot, orecv, aysend, attp,
     kvsend, dqsend, dqt, dka, dva, dl,
-    gwp, s1recv, s2send, s2recv, piece, psend, precv,
+    gwp, s0recv, s1recv, s2send, s2recv, piece, psend, precv,
     qkv_s, qkv_r, do_s, do_r, o_s, o_r, kv_s, kv_r, dq_s, dq_r,
     c_s, c_r, dy_s, dy_r, ay_s, ay_r, p_s, p_r,
-    w1_s, w1_r, w2_s, w2_r, w3_s, w3_r, g1_s, g1_r, g2_s, g2_r, g3_s, g3_r,
+    w1_s, w1_r, w2_s, w2_r, w3_s, w3_r, g0_s, g0_r, g1_s, g1_r, g2_s, g2_r, g3_s, g3_r,
 ):
     d, me = place()
     y, zl = d // NZL, d % NZL
     x, zh, core = me // (2 * NZH), (me // 2) % NZH, me % 2
-    xc, zz = x * 2 + core, zh * NZL + zl
+    zz = zh * NZL + zl
     tok, width = q_ref.shape
     half = tok // 2
     blocks = send.shape[0]
@@ -141,9 +141,12 @@
     def dq_copy(t, src):
         return remote(dqsend.at[t], dqrecv.at[src], dq_s.at[t], dq_r.at[src], (d, t))
 
+    def g0_copy(c):
+        return remote(gwp.at[al(c, group), :], s0recv, g0_s.at[0], g0_r.at[0], (d, seq_of(x, zh, 1 - core)))
+
     def g1_copy(t, src):
-        rows = pl.ds(pl.multiple_of((t % 2) * group + (t // 2) * NZH * per, NZH * per), NZH * per)
-        dev = (d, seq_of(t // 2, zh, t % 2))
+        rows = pl.ds(pl.multiple_of(core * group + t * NZH * per, NZH * per), NZH * per)
+        dev = (d, seq_of(t, zh, core))
         return remote(gwp.at[rows, :], s1recv.at[src], g1_s.at[t], g1_r.at[src], dev)
 
     def g2_copy(t, src):
@@ -224,6 +227,25 @@
         unpack(t)
         return c
 
+    def regroup(i, c):
+        t = (me + i) % blocks
+        rows = pl.ds(pl.multiple_of((t // 2) * per, per), per)
+        for b in range(NY):
+            dosend[t, b * per : (b + 1) * per, :] = dyrecv[t % 2, b, rows, :]
+
+        @pl.when(t != me)
+        def _():
+            do_copy(t, me).start()
+
+        @pl.when(t == me)
+        def _():
+            dot[:, al(t, tok)] = dosend[t]
+
+        return c
+
+    for c in range(2):
+        others(NY, y, lambda t: dy_copy(c, t, t).wait_recv())
+    lax.fori_loop(0, blocks, regroup, 0)
     unpack(me)
     lax.fori_loop(1, 2 * NZH, near_in, 0)
     lax.fori_loop(0, (NX - 1) * 2 * NZH, far_in, 0)
@@ -269,22 +291,6 @@
         @pl.when((last - first) % 2 == 1)
         def _():
             body(last - 1)
-
-    def regroup(i, c):
-        t = (me + i) % blocks
-        rows = pl.ds(pl.multiple_of((t // 2) * per, per), per)
-        for b in range(NY):
-            dosend[t, b * per : (b + 1) * per, :] = dyrecv[t % 2, b, rows, :]
-
-        @pl.when(t != me)
-        def _():
-            do_copy(t, me).start()
-
-        @pl.when(t == me)
-        def _():
-            dot[:, al(t, tok)] = dosend[t]
-
-        return c
 
     def qblock(i, c):
         b = (i + me) % steps
@@ -324,12 +330,6 @@
             @pl.when(t == me)
             def _():
                 orecv[t] = ot[:, al(t, tok)]
-
-        @pl.when(i == 0)
-        def _():
-            for c in range(2):
-                others(NY, y, lambda t: dy_copy(c, t, t).wait_recv())
-            lax.fori_loop(0, blocks, regroup, 0)
 
         return c
 
@@ -411,7 +411,13 @@
             for g in range(width // 512):
                 cols = slice(g * 512, (g + 1) * 512)
                 gwp[:, cols] = dg(attp[...], cotg[:, cols], 1, 0).astype(bf)
-            others(2 * NX, xc, lambda t: g1_copy(t, xc).start())
+            g0_copy(1 - core).start()
+            g0_copy(1 - core).wait_recv()
+            for n in range(group // 32):
+                rows = pl.ds(pl.multiple_of(core * group + n * 32, 32), 32)
+                both = gwp[rows, :].astype(f32) + s0recv[n * 32 : (n + 1) * 32, :].astype(f32)
+                gwp[rows, :] = both.astype(bf)
+            others(NX, x, lambda t: g1_copy(t, x).start())
 
         @pl.when(i == 2)
         def _():
@@ -421,16 +427,16 @@
                 psend[b] = part.astype(bf)
             others(NY, y, lambda t: p_copy(t, y).start())
 
-        @pl.when(i == 5)
-        def _():
-            others(2 * NX, xc, lambda t: g1_copy(t, t).wait_recv())
-            s1recv[xc] = gwp[
+        @pl.when(i == 4)
+        def _():
+            others(NX, x, lambda t: g1_copy(t, t).wait_recv())
+            s1recv[x] = gwp[
                 pl.ds(pl.multiple_of(core * group + x * NZH * per, NZH * per), NZH * per), :
             ]
             size = per // NZL
             for n in range(NZH * NZL):
                 total = s1recv[0, n * size : (n + 1) * size, :].astype(f32)
-                for m in range(1, 2 * NX):
+                for m in range(1, NX):
                     total = total + s1recv[m, n * size : (n + 1) * size, :].astype(f32)
                 s2send[n] = total.astype(bf)
             others(NZH * NZL, zz, lambda t: g2_copy(t, zz).start())
@@ -487,7 +493,8 @@
     others(NZH, zh, lambda t: w1_copy(t, zh).wait_send())
     others(NX, x, lambda t: w2_copy(t, x).wait_send())
     w3_copy(core).wait_send()
-    others(2 * NX, xc, lambda t: g1_copy(t, xc).wait_send())
+    g0_copy(1 - core).wait_send()
+    others(NX, x, lambda t: g1_copy(t, x).wait_send())
     others(NZH * NZL, zz, lambda t: g2_copy(t, zz).wait_send())
     others(dps, d, lambda t: g3_copy(t, d).wait_send())
 
@@ -566,7 +573,8 @@
             vmem((QB, HS), f32),
             vmem((1, length), f32),
             vmem((group * per, width), bf),
-            vmem((2 * NX, NZH * per, width), bf),
+            vmem((group // 2 * per, width), bf),
+            vmem((NX, NZH * per, width), bf),
             vmem((NZH * NZL, per // NZL, width), bf),
             vmem((NZH * NZL, per // NZL, width), bf),
             vmem((per // NZL, width), f32),
@@ -584,7 +592,8 @@
             *sems(NZH),
             *sems(NX),
             *sems(1),
-            *sems(2 * NX),
+            *sems(1),
+            *sems(NX),
             *sems(NZH * NZL),
             *sems(NY * NZL),
         ],

time: 167 us -> 163 us (0.976)
  Pallas kernels: 166 us -> 162 us
    pallas_call x1, Pallas kernels: 162 us -> 158 us  [on_device(): pl.pallas_call(kernel, out_shape=(sds((tok, width), bf), sds((group, tok,...]
where the time goes in v6:
time: 163 us; the launch traced here: 162 us
  Pallas kernels  162 us (99%)
    pallas_call x1, Pallas kernels, on_device(): pl.pallas_call(kernel, out_shape=(sds((tok, width), bf), sds((group, tok,...  158 us
    pallas_call x1, Pallas kernels, on_device(): pl.pallas_call(finish_kernel, out_shape=(sds((tok, width), bf),) * 4 + (s...  4.05 us

profile of v6, /device:TPU:1, one launch (start us, length us, event | category | flops | bytes accessed | tf_op | source)
XLA Modules:
  0.0 162.2 jit_solution(10643883446323562148)
XLA Ops:
  0.6 157.5 %attention_step.1 = (bf16[128,2048]{1,0:T(8,128)(2,1)}, bf16[32,128,128]{2,1,0:T(8,128)(2,1)}, bf16[32,64,128]{2,1,0:T(8,128)(2,1)}, f32[64,2048]{1,0:T(8,128)}) custom-call(bf16[128,2048]{1,0:T(8,128)(2,1)} %bitcast.8, bf16[128,2048]{1,0:T(8,128)(2,1)} %bitcast.9, bf16[128,2048]{1,0:T(8,128)(2,1)} %bitcast.10, s32[1,128]{1,0:T(1,128)} %frame_hbm.1, ...), custom_call_target="tpu_custom_call" | custom-call | tf_op jit(solution)/shard_map/attention_step/pallas_call | solution.py:529
  158.2 4.1 %finish.1 = (bf16[128,2048]{1,0:T(8,128)(2,1)}, bf16[128,2048]{1,0:T(8,128)(2,1)}, bf16[128,2048]{1,0:T(8,128)(2,1)}, bf16[128,2048]{1,0:T(8,128)(2,1)}, f32[64,2048]{1,0:T(8,128)}) custom-call(bf16[128,2048]{1,0:T(8,128)(2,1)} %get-tuple-element.14.out_in, bf16[32,128,128]{2,1,0:T(8,128)(2,1)} %get-tuple-element.15.kvrecv, ...), custom_call_target="tpu_custom_call" | custom-call | tf_op jit(solution)/shard_map/finish/pallas_call | solution.py:605
